TPU v7x, 512 devices: a whole 4x8x8 slice. The times are simulated.
512 devices in a mesh: branch: 2 (over y_hi), ctx: 32 (over x, y_lo, core), tp: 8 (over z).
Axes of the slice: x: 4, y: 8 (y_hi: 2, y_lo: 4; y = y_hi * 4 + y_lo), z: 8, core: 2. Of those that a mesh axis runs over, the one named last changes fastest.
Arguments:
- queries: bfloat16 [2, 8192, 8192], P('branch', 'ctx', 'tp'), may hold values from -12 to 12
- keys: bfloat16 [2, 8192, 1024], P('branch', 'ctx', 'tp'), may hold values from -12 to 12
- values: bfloat16 [2, 8192, 1024], P('branch', 'ctx', 'tp'), may hold values from -800 to 800
- segments: int32 [8192], replicated, may hold values from 0 to 3, never falling along the last dimension, each value on 1 to 4096 neighbouring positions
- norm_gain: float32 [2, 8192], P('branch', 'tp'), may hold values from 0.5 to 1.5
- head_weight: float32 [2, 8192], P('branch', 'tp'), may hold values from -0.0625 to 0.0625
Outputs:
- normed: bfloat16 [2, 8192, 8192], P('branch', 'ctx', 'tp')
- joined: float32 [8192], P('ctx')
Inputs may be any that keep to these rules, and one draw needn't show every extreme that they name: `segments`: rollout ids never fall along the sequence; each rollout holds 1 to 4096 tokens, and one holds exactly 4096.
All inputs are finite; a program needn't handle non-finite values.
Results may differ from a plain program's by a relative error of at most 0.007.
Values may be sent and summed in bfloat16 or wider, within the bound.
No kernel may reach another device: no remote copies, remote signals or barrier semaphores. Data moves between devices by JAX's collectives and lax.ppermute only.
A program may use at most 64 MiB of HBM per device.

v0:
```python
import functools
import math

import jax
import jax.numpy as jnp
from jax import lax
from jax.experimental import pallas as pl
from jax.experimental.pallas import tpu as pltpu
from jax.sharding import PartitionSpec as P


HD = 128
D = 8192
NEGATIVE = -1e30
EPSILON = 1e-06

NX, NY = 4, 4
AHEAD, BEHIND = 2, 1


VMEM = pl.BlockSpec(memory_space=pltpu.VMEM)
SMEM = pl.BlockSpec(memory_space=pltpu.SMEM)


def unpack(d):
    return d // (2 * NY), (d // 2) % NY, d % 2


def pack(x, y, core):
    return (x * NY + y) * 2 + core


def moved(block, target):
    route = []
    for d in range(2 * NX * NY):
        x, y, core = target(*unpack(d))
        if 0 <= x < NX and 0 <= y < NY:
            route.append((d, pack(x, y, core)))
    return lax.ppermute(block, "ctx", route)


def attend_kernel(plan, first, last, members, *refs):
    if first:
        here_ref, segments_ref, q_ref = refs[:3]
        refs = refs[3:]
    else:
        meta_ref, q_ref = refs[:2]
        refs = refs[2:]
    kv_refs, refs = refs[: len(plan)], refs[len(plan) :]
    if not first:
        m_in, l_in, acc_in = refs[:3]
        refs = refs[3:]
    if last:
        gain_ref, weight_ref = refs[:2]
        att_ref, stats_ref, m_ref, l_ref, acc_ref = refs[2:]
    elif first:
        meta_ref, m_ref, l_ref, acc_ref = refs
    else:
        m_ref, l_ref, acc_ref = refs
    rows = q_ref.shape[0]
    heads = q_ref.shape[1] // HD
    keys = kv_refs[0].shape[2]
    factor = math.log2(math.e) / math.sqrt(HD)

    if first:
        here = here_ref[0]
        segments = segments_ref[...]
        meta_ref[0] = here
        bounds = []
        for s in (1, 2, 3):
            ahead = jnp.sum((segments < s).astype(jnp.float32)).astype(jnp.int32)
            meta_ref[s] = ahead
            bounds.append(ahead)
    else:
        here = meta_ref[0]
        bounds = [meta_ref[s] for s in (1, 2, 3)]
    x, y, core = here >> 3, (here >> 1) & (NY - 1), here & 1
    first_row = here * rows

    def start_of(position):
        start = jnp.zeros_like(position)
        for bound in bounds:
            start = jnp.maximum(start, jnp.where(bound <= position, bound, 0))
        return start

    low, high = start_of(first_row), start_of(first_row + rows - 1)

    if first:
        m_ref[...] = jnp.full_like(m_ref, NEGATIVE)
        l_ref[...] = jnp.zeros_like(l_ref)
        acc_ref[...] = jnp.zeros_like(acc_ref)
    else:
        m_ref[...] = m_in[...]
        l_ref[...] = l_in[...]
        acc_ref[...] = acc_in[...]

    def visit(key_rows, value_rows, offset, masked):
        tall = jnp.concatenate([value_rows.T, jnp.ones((16, keys), jnp.bfloat16)], axis=0)
        if masked:
            key_pos = offset + lax.broadcasted_iota(jnp.int32, (keys, rows), 0)
            query_pos = first_row + lax.broadcasted_iota(jnp.int32, (1, rows), 1)
            allowed = (key_pos >= start_of(query_pos)) & (key_pos <= query_pos)

        def scores_of(g):
            return lax.dot_general(
                key_rows,
                q_ref[:, g * HD : (g + 1) * HD],
                (((1,), (1,)), ((), ())),
                preferred_element_type=jnp.float32,
            )

        def mix(g, weights, rescale):
            mixed = jnp.dot(tall, weights, preferred_element_type=jnp.float32)
            l_ref[g] = l_ref[g] * rescale + mixed[HD : HD + 8]
            held = acc_ref[g].reshape(HD // 8, 8, rows) * rescale[None]
            acc_ref[g] = held.reshape(HD, rows) + mixed[:HD]

        ready = {g: scores_of(g) for g in range(min(AHEAD, heads))}
        waiting = []
        for g in range(heads):
            if g + AHEAD < heads:
                ready[g + AHEAD] = scores_of(g + AHEAD)
            scores = ready.pop(g)
            if masked:
                scores = jnp.where(allowed, scores, NEGATIVE)
            scores = scores.reshape(keys // 8, 8, rows)
            old = m_ref[g]
            top = jnp.max(jnp.max(scores, axis=0), axis=0, keepdims=True)
            new = jnp.maximum(old, jnp.broadcast_to(top, old.shape))
            m_ref[g] = new
            rescale = jnp.exp2((old - new) * factor)
            weights = jnp.exp2((scores - new[None]) * factor)
            waiting.append((g, weights.reshape(keys, rows).astype(jnp.bfloat16), rescale))
            if len(waiting) > BEHIND:
                mix(*waiting.pop(0))
        for entry in waiting:
            mix(*entry)

    for kv_ref, (count, shift, across, flip) in zip(kv_refs, plan):

        def one(i, carry, kv_ref=kv_ref, count=count, shift=shift, across=across, flip=flip):
            j = count - 1 - i
            if shift is not None:
                yy, xx = y, x + shift + j
            else:
                other = across if isinstance(across, int) else jnp.where(j < 2, *across)
                yy = jnp.bitwise_xor(y, other)
                xx = jnp.where(yy < y, x - 1, x - 2) + (j & 1)
            offset = (((xx * NY + yy) * 2) + jnp.bitwise_xor(core, flip)) * rows
            valid = (xx >= 0) & (offset <= first_row) & (offset + keys > low)
            clear = (offset >= high) & (offset + keys <= first_row)

            if not first:

                @pl.when(valid & clear)
                def _():
                    visit(kv_ref[j, 0], kv_ref[j, 1], offset, False)

            @pl.when(valid if first else valid & ~clear)
            def _():
                visit(kv_ref[j, 0], kv_ref[j, 1], offset, True)

            return carry

        lax.fori_loop(0, count, one, 0)

    if last:
        squares = jnp.zeros((8, rows), jnp.float32)
        dotted = jnp.zeros((8, rows), jnp.float32)
        product = gain_ref[...] * weight_ref[...]
        pieces = []
        for _ in range(3):
            pieces.append(product.astype(jnp.bfloat16))
            product = product - pieces[-1].astype(jnp.float32)
        pieces = jnp.concatenate(
            [p.astype(jnp.float32) for p in pieces] + [jnp.zeros((5, product.shape[1]), jnp.float32)],
            axis=0,
        ).astype(jnp.bfloat16)
        for g in range(heads):
            part = acc_ref[g].reshape(HD // 8, 8, rows) / l_ref[g][None]
            attended = part.reshape(HD, rows).astype(jnp.bfloat16)
            att_ref[g] = attended
            wide = attended.astype(jnp.float32)
            squares += jnp.sum((wide * wide).reshape(HD // 8, 8, rows), axis=0)
            dotted += jnp.dot(
                pieces[:, g * HD : (g + 1) * HD], attended, preferred_element_type=jnp.float32
            )
        line = jnp.concatenate(
            [jnp.sum(v, axis=0, keepdims=True) for v in (squares, dotted)], axis=1
        )
        for i in range(members):
            stats_ref[i] = line


SMALL = pltpu.CompilerParams(vmem_limit_bytes=16 * 1024 * 1024)


def attend(operands, blocks, plan, state=None, gains=None, members=0):
    first, last = state is None, gains is not None
    rows, width = operands[-1].shape
    heads = width // HD
    state_shapes = [(heads, 8, rows), (heads, 8, rows), (heads, HD, rows)]
    operands = [*operands, *blocks, *(state or ()), *(gains or ())]
    scratch = []
    if last:
        out_shape = (
            jax.ShapeDtypeStruct((heads, HD, rows), jnp.bfloat16),
            jax.ShapeDtypeStruct((members, 1, 2 * rows), jnp.float32),
        )
        out_specs = (VMEM, VMEM)
        scratch = [pltpu.VMEM(s, jnp.float32) for s in state_shapes]
    else:
        out_shape = tuple(jax.ShapeDtypeStruct(s, jnp.float32) for s in state_shapes)
        out_specs = (VMEM,) * 3
        if first:
            out_shape = (jax.ShapeDtypeStruct((4,), jnp.int32),) + out_shape
            out_specs = (SMEM,) + out_specs
    pairs = sum(p[0] for p in plan) * blocks[0].shape[2] * rows * heads
    return pl.pallas_call(
        functools.partial(attend_kernel, plan, first, last, members),
        out_shape=out_shape,
        in_specs=[SMEM] + [VMEM] * (len(operands) - 1),
        out_specs=out_specs,
        scratch_shapes=scratch,
        compiler_params=SMALL,
        cost_estimate=pl.CostEstimate(
            flops=4 * pairs * HD, bytes_accessed=4 * rows * width, transcendentals=pairs
        ),
        name="attend",
    )(*operands)


def prepare_kernel(att_ref, gain_ref, out_ref):
    heads = att_ref.shape[0]
    for g in range(heads):
        at = slice(g * HD, (g + 1) * HD)
        out_ref[:, at] = att_ref[g].astype(jnp.float32).T * gain_ref[:, at]


def finish_kernel(branches, mine_ref, everyone, scaled_ref, normed_ref, joined_ref):
    rows, width = scaled_ref.shape
    size = everyone.shape[0] // branches
    mine = mine_ref[0]
    joined = jnp.zeros((1, rows), jnp.float32)
    own = jnp.zeros((1, rows), jnp.float32)
    for b in range(branches):
        total = everyone[b * size]
        for i in range(1, size):
            total = total + everyone[b * size + i]
        inverse = lax.rsqrt(total[:, :rows] / D + EPSILON)
        joined += inverse * total[:, rows:]
        own = jnp.where(mine == b, inverse, own)
    joined_ref[...] = joined
    tall = jnp.broadcast_to(own, (HD, rows)).T
    for g in range(width // HD):
        at = slice(g * HD, (g + 1) * HD)
        normed_ref[:, at] = (scaled_ref[:, at] * tall).astype(jnp.bfloat16)


def local(queries, keys, values, segments, norm_gain, head_weight):
    rows = queries.shape[1]
    here = lax.axis_index("ctx")
    y = (here >> 1) & (NY - 1)
    q = queries[0]
    rows, width = q.shape

    own = jnp.stack([keys[0], values[0]])[None]
    partner = lambda b: moved(b, lambda x, y, c: (x, y, c ^ 1))
    from_1 = moved(own, lambda x, y, c: (x + 1, y, c))
    from_2 = moved(own, lambda x, y, c: (x + 2, y, c))

    meta, *state = attend(
        [here.reshape(1), segments.reshape(-1, HD), q], [own], ((1, 0, 0, 0),)
    )
    column = jnp.concatenate([from_2, from_1, own])
    pick = lambda up: jnp.where(up, column[1:], column[:2])
    across_2 = moved(pick(y < 2), lambda x, y, c: (x, y ^ 2, c))
    across_1 = moved(pick((y & 1) == 0), lambda x, y, c: (x, y ^ 1, c))
    column_p = partner(column)
    state = attend([meta, q], [column, column_p], ((2, -2, 0, 0), (3, -2, 0, 1)), state)
    state = attend([meta, q], [across_1], ((2, None, 1, 0),), state)
    across_3 = moved(across_2, lambda x, y, c: (x, y ^ 1, c))
    near = jnp.concatenate([across_1, across_2])
    near_p = partner(near)
    state = attend([meta, q], [across_2], ((2, None, 2, 0),), state)
    state = attend([meta, q], [near_p], ((4, None, (1, 2), 1),), state)
    across_3p = partner(across_3)
    state = attend([meta, q], [across_3], ((2, None, 3, 0),), state)
    branches = lax.axis_size("branch")
    members = branches * lax.axis_size("tp")
    attended, stats = attend(
        [meta, q],
        [across_3p],
        ((2, None, 3, 1),),
        state,
        (norm_gain, head_weight),
        members,
    )
    everyone = lax.all_to_all(stats, ("branch", "tp"), 0, 0, tiled=True)
    scaled = pl.pallas_call(
        prepare_kernel,
        out_shape=jax.ShapeDtypeStruct((rows, width), jnp.float32),
        in_specs=[VMEM] * 2,
        out_specs=VMEM,
        compiler_params=SMALL,
        name="prepare",
    )(attended, norm_gain)
    normed, joined = pl.pallas_call(
        functools.partial(finish_kernel, branches),
        out_shape=(
            jax.ShapeDtypeStruct((rows, width), jnp.bfloat16),
            jax.ShapeDtypeStruct((1, rows), jnp.float32),
        ),
        in_specs=[SMEM] + [VMEM] * 2,
        out_specs=(VMEM,) * 2,
        compiler_params=SMALL,
        name="finish",
    )(lax.axis_index("branch").reshape(1), everyone, scaled)
    return (normed[None], joined[0])


def solution(mesh):
    return jax.shard_map(
        local,
        mesh=mesh,
        in_specs=(
            P("branch", "ctx", "tp"),
            P("branch", "ctx", "tp"),
            P("branch", "ctx", "tp"),
            P(),
            P("branch", "tp"),
            P("branch", "tp"),
        ),
        out_specs=(P("branch", "ctx", "tp"), P("ctx")),
        check_vma=False,
    )
```

profile of v0, /device:TPU:31, one launch (start us, length us, event | category | flops | bytes accessed | tf_op | source)
XLA Modules:
  0.0 89.8 jit_solution(15870163716039734876)
XLA Ops:
  0.6 0.9 maximum_bitcast_fusion.refs_3_
  1.5 1.3 %collective-permute-start.1 = (bf16[1,2,256,128]{3,2,1,0:T(8,128)(2,1)S(1)}, bf16[1,2,256,128]{3,2,1,0:T(8,128)(2,1)S(1)}, u32[]{:S(2)}, u32[]{:S(2)}) collective-permute-start(bf16[1,2,256,128]{3,2,1,0:T(8,128)(2,1)S(1)} %maximum_bitcast_fusion.refs_3_), channel_id=1, source_target_pairs={{0,128},{8,136},{16,144},{24,152},{32,160},{40,168},{48,176},{56,1... | collective-permute-start | bytes 393224 | tf_op jit(solution)/shard_map/ppermute | solution.py:39
  2.8 1.3 %collective-permute-start = (bf16[1,2,256,128]{3,2,1,0:T(8,128)(2,1)S(1)}, bf16[1,2,256,128]{3,2,1,0:T(8,128)(2,1)S(1)}, u32[]{:S(2)}, u32[]{:S(2)}) collective-permute-start(bf16[1,2,256,128]{3,2,1,0:T(8,128)(2,1)S(1)} %maximum_bitcast_fusion.refs_3_), channel_id=1, source_target_pairs={{0,64},{8,72},{16,80},{24,88},{32,96},{40,104},{48,112},{56,120},{... | collective-permute-start | bytes 393224 | tf_op jit(solution)/shard_map/ppermute | solution.py:39
  4.1 5.2 %collective-permute-done.1 = bf16[1,2,256,128]{3,2,1,0:T(8,128)(2,1)S(1)} collective-permute-done((bf16[1,2,256,128]{3,2,1,0:T(8,128)(2,1)S(1)}, bf16[1,2,256,128]{3,2,1,0:T(8,128)(2,1)S(1)}, u32[]{:S(2)}, u32[]{:S(2)}) %collective-permute-start.1) | collective-permute-done | bytes 131104 | tf_op jit(solution)/shard_map/ppermute | solution.py:39
  9.3 0.0 collective-permute-done
  9.4 2.1 %collective-permute-start.5 = (bf16[2,2,256,128]{3,2,1,0:T(8,128)(2,1)S(1)}, bf16[2,2,256,128]{3,2,1,0:T(8,128)(2,1)S(1)}, u32[]{:S(2)}, u32[]{:S(2)}) collective-permute-start(bf16[2,2,256,128]{3,2,1,0:T(8,128)(2,1)S(1)} %get-tuple-element.48), channel_id=1, source_target_pairs={{0,16},{8,24},{16,0},{24,8},{32,48},{40,56},{48,32},{56,40},{64,80... | collective-permute-start | bytes 786440 | tf_op jit(solution)/shard_map/ppermute | solution.py:39
  11.5 2.0 %collective-permute-start.2 = (bf16[2,2,256,128]{3,2,1,0:T(8,128)(2,1)S(1)}, bf16[2,2,256,128]{3,2,1,0:T(8,128)(2,1)S(1)}, u32[]{:S(2)}, u32[]{:S(2)}) collective-permute-start(bf16[2,2,256,128]{3,2,1,0:T(8,128)(2,1)S(1)} %get-tuple-element.49), channel_id=1, source_target_pairs={{0,32},{8,40},{16,48},{24,56},{32,0},{40,8},{48,16},{56,24},{64,96... | collective-permute-start | bytes 786440 | tf_op jit(solution)/shard_map/ppermute | solution.py:39
  13.5 0.0 copy-start.1
  13.5 0.0 copy-start.2
  13.5 4.1 %collective-permute-start.7 = (bf16[3,2,256,128]{3,2,1,0:T(8,128)(2,1)S(1)}, bf16[3,2,256,128]{3,2,1,0:T(8,128)(2,1)S(1)}, u32[]{:S(2)}, u32[]{:S(2)}) collective-permute-start(bf16[3,2,256,128]{3,2,1,0:T(8,128)(2,1)S(1)} %pad_maximum_fusion.1.refs_2_), channel_id=1, source_target_pairs={{0,8},{8,0},{16,24},{24,16},{32,40},{40,32},{48,56},{56,48},{64,72... | collective-permute-start | bytes 1179656 | tf_op jit(solution)/shard_map/ppermute | solution.py:39
  17.7 1.5 %collective-permute-done.5.refs_2_ = bf16[2,2,256,128]{3,2,1,0:T(8,128)(2,1)S(1)} collective-permute-done((bf16[2,2,256,128]{3,2,1,0:T(8,128)(2,1)S(1)}, bf16[2,2,256,128]{3,2,1,0:T(8,128)(2,1)S(1)}, u32[]{:S(2)}, u32[]{:S(2)}) %collective-permute-start.5) | collective-permute-done | bytes 262176 | tf_op jit(solution)/shard_map/ppermute | solution.py:39
  19.2 7.5 %collective-permute-done.2.refs_2_ = bf16[2,2,256,128]{3,2,1,0:T(8,128)(2,1)S(1)} collective-permute-done((bf16[2,2,256,128]{3,2,1,0:T(8,128)(2,1)S(1)}, bf16[2,2,256,128]{3,2,1,0:T(8,128)(2,1)S(1)}, u32[]{:S(2)}, u32[]{:S(2)}) %collective-permute-start.2) | collective-permute-done | bytes 262176 | tf_op jit(solution)/shard_map/ppermute | solution.py:39
  26.7 3.9 %collective-permute-start.6 = (bf16[4,2,256,128]{3,2,1,0:T(8,128)(2,1)S(1)}, bf16[4,2,256,128]{3,2,1,0:T(8,128)(2,1)S(1)}, u32[]{:S(2)}, u32[]{:S(2)}) collective-permute-start(bf16[4,2,256,128]{3,2,1,0:T(8,128)(2,1)S(1)} %pad_maximum_fusion), channel_id=1, source_target_pairs={{0,8},{8,0},{16,24},{24,16},{32,40},{40,32},{48,56},{56,48},{64,72... | collective-permute-start | bytes 1572872 | tf_op jit(solution)/shard_map/ppermute | solution.py:39
  30.6 1.9 %collective-permute-start.3 = (bf16[2,2,256,128]{3,2,1,0:T(8,128)(2,1)S(1)}, bf16[2,2,256,128]{3,2,1,0:T(8,128)(2,1)S(1)}, u32[]{:S(2)}, u32[]{:S(2)}) collective-permute-start(bf16[2,2,256,128]{3,2,1,0:T(8,128)(2,1)S(1)} %collective-permute-done.2.refs_2_), channel_id=1, source_target_pairs={{0,16},{8,24},{16,0},{24,8},{32,48},{40,56},{48,32},{56,40},{64,80... | collective-permute-start | bytes 786440 | tf_op jit(solution)/shard_map/ppermute | solution.py:39
  32.6 1.9 %attend.7 = (s32[4]{0:T(128)S(1)}, f32[8,8,256]{2,1,0:T(8,128)S(1)}, f32[8,8,256]{2,1,0:T(8,128)S(1)}, f32[8,128,256]{2,1,0:T(8,128)S(1)}) custom-call(s32[1]{0:T(128)} %bitcast.1.refs_0_, s32[64,128]{1,0:T(8,128)S(1)} %bitcast.15, bf16[256,1024]{1,0:T(8,128)(2,1)S(1)} %bitcast.8, bf16[1,2,256,128]{3,2,1,0:T(8,128)(2,1)S(1)} %maximum_bitcast_fusion.refs_3_), custom_call_target="tpu_custom_call" | custom-call | flops 268435456 | bytes 1048576 | tf_op jit(solution)/shard_map/attend/pallas_call | solution.py:219
  34.5 5.9 %collective-permute-done.3.refs_2_ = bf16[2,2,256,128]{3,2,1,0:T(8,128)(2,1)S(1)} collective-permute-done((bf16[2,2,256,128]{3,2,1,0:T(8,128)(2,1)S(1)}, bf16[2,2,256,128]{3,2,1,0:T(8,128)(2,1)S(1)}, u32[]{:S(2)}, u32[]{:S(2)}) %collective-permute-start.3) | collective-permute-done | bytes 262176 | tf_op jit(solution)/shard_map/ppermute | solution.py:39
  40.4 2.8 %collective-permute-start.4 = (bf16[2,2,256,128]{3,2,1,0:T(8,128)(2,1)S(1)}, bf16[2,2,256,128]{3,2,1,0:T(8,128)(2,1)S(1)}, u32[]{:S(2)}, u32[]{:S(2)}) collective-permute-start(bf16[2,2,256,128]{3,2,1,0:T(8,128)(2,1)S(1)} %collective-permute-done.3.refs_2_), channel_id=1, source_target_pairs={{0,8},{8,0},{16,24},{24,16},{32,40},{40,32},{48,56},{56,48},{64,72... | collective-permute-start | bytes 786440 | tf_op jit(solution)/shard_map/ppermute | solution.py:39
  43.2 0.0 collective-permute-done.7.refs_3_
  43.2 3.7 %attend.8 = (f32[8,8,256]{2,1,0:T(8,128)S(1)}, f32[8,8,256]{2,1,0:T(8,128)S(1)}, f32[8,128,256]{2,1,0:T(8,128)S(1)}) custom-call(s32[4]{0:T(128)S(1)} %get-tuple-element.25.refs_0_, bf16[256,1024]{1,0:T(8,128)(2,1)S(1)} %bitcast.9, bf16[3,2,256,128]{3,2,1,0:T(8,128)(2,1)S(1)} %pad_maximum_fusion.1.refs_2_, ...), custom_call_target="tpu_custom_call" | custom-call | flops 1342177280 | bytes 1048576 | tf_op jit(solution)/shard_map/attend/pallas_call | solution.py:219
  46.9 2.6 %attend.9 = (f32[8,8,256]{2,1,0:T(8,128)S(1)}, f32[8,8,256]{2,1,0:T(8,128)S(1)}, f32[8,128,256]{2,1,0:T(8,128)S(1)}) custom-call(s32[4]{0:T(128)S(1)} %get-tuple-element.25.refs_0_, bf16[256,1024]{1,0:T(8,128)(2,1)S(1)} %bitcast.10, bf16[2,2,256,128]{3,2,1,0:T(8,128)(2,1)S(1)} %collective-permute-done.5.refs_2_, f32[8,8,256]{2,1,0:T(8,128)S(1)} %get-tuple-element.29.refs_3_, ...), custom_call_target="tpu_custom_call" | custom-call | flops 536870912 | bytes 1048576 | tf_op jit(solution)/shard_map/attend/pallas_call | solution.py:219
  49.5 2.6 %attend.10 = (f32[8,8,256]{2,1,0:T(8,128)S(1)}, f32[8,8,256]{2,1,0:T(8,128)S(1)}, f32[8,128,256]{2,1,0:T(8,128)S(1)}) custom-call(s32[4]{0:T(128)S(1)} %get-tuple-element.25.refs_0_, bf16[256,1024]{1,0:T(8,128)(2,1)S(1)} %bitcast.11, bf16[2,2,256,128]{3,2,1,0:T(8,128)(2,1)S(1)} %collective-permute-done.2.refs_2_, ...), custom_call_target="tpu_custom_call" | custom-call | flops 536870912 | bytes 1048576 | tf_op jit(solution)/shard_map/attend/pallas_call | solution.py:219
  52.2 4.7 %attend.11 = (f32[8,8,256]{2,1,0:T(8,128)S(1)}, f32[8,8,256]{2,1,0:T(8,128)S(1)}, f32[8,128,256]{2,1,0:T(8,128)S(1)}) custom-call(s32[4]{0:T(128)S(1)} %get-tuple-element.25.refs_0_, bf16[256,1024]{1,0:T(8,128)(2,1)S(1)} %bitcast.12, bf16[4,2,256,128]{3,2,1,0:T(8,128)(2,1)S(1)} %collective-permute-done.6.refs_2_, ...), custom_call_target="tpu_custom_call" | custom-call | flops 1073741824 | bytes 1048576 | tf_op jit(solution)/shard_map/attend/pallas_call | solution.py:219
  56.9 0.0 copy-start.3
  56.9 2.6 %attend.12 = (f32[8,8,256]{2,1,0:T(8,128)S(1)}, f32[8,8,256]{2,1,0:T(8,128)S(1)}, f32[8,128,256]{2,1,0:T(8,128)S(1)}) custom-call(s32[4]{0:T(128)S(1)} %get-tuple-element.25.refs_0_, bf16[256,1024]{1,0:T(8,128)(2,1)S(1)} %bitcast.13, bf16[2,2,256,128]{3,2,1,0:T(8,128)(2,1)S(1)} %collective-permute-done.3.refs_2_, ...), custom_call_target="tpu_custom_call" | custom-call | flops 536870912 | bytes 1048576 | tf_op jit(solution)/shard_map/attend/pallas_call | solution.py:219
  59.5 0.0 copy-start
  59.5 0.0 collective-permute-done.4.refs_2_
  59.6 0.7 copy-done
  60.2 3.7 %attend.13 = (bf16[8,128,256]{2,1,0:T(8,128)(2,1)S(1)}, f32[16,1,512]{2,1,0:T(1,128)}) custom-call(s32[4]{0:T(128)S(1)} %get-tuple-element.25.refs_0_, bf16[256,1024]{1,0:T(8,128)(2,1)S(1)} %bitcast.14, bf16[2,2,256,128]{3,2,1,0:T(8,128)(2,1)S(1)} %collective-permute-done.4.refs_2_, f32[8,8,256]{2,1,0:T(8,128)S(1)} %get-tuple-element.41.refs_3_, ...), custom_call_target="tpu_custom_call" | custom-call | flops 536870912 | bytes 1048576 | tf_op jit(solution)/shard_map/attend/pallas_call | solution.py:219
  64.0 13.6 %all-to-all-start = ((f32[16,1,512]{2,1,0:T(1,128)}), f32[16,1,512]{2,1,0:T(1,128)S(1)}, u32[]{:S(2)}, u32[]{:S(2)}) async-start(f32[16,1,512]{2,1,0:T(1,128)} %get-tuple-element.44), calls=%async_computation | async-start | bytes 65536 | tf_op jit(solution)/shard_map/all_to_all | solution.py:299
  77.6 0.2 prepare.1.scaled_ref
  77.8 11.1 %all-to-all-done.everyone = f32[16,1,512]{2,1,0:T(1,128)S(1)} async-done(((f32[16,1,512]{2,1,0:T(1,128)}), f32[16,1,512]{2,1,0:T(1,128)S(1)}, u32[]{:S(2)}, u32[]{:S(2)}) %all-to-all-start) | async-done | bytes 32800 | tf_op jit(solution)/shard_map/all_to_all | solution.py:299
  88.9 1.0 %finish.1 = (bf16[256,1024]{1,0:T(8,128)(2,1)}, f32[1,256]{1,0:T(1,128)}) custom-call(s32[1]{0:T(128)} %bitcast.mine_ref, f32[16,1,512]{2,1,0:T(1,128)S(1)} %all-to-all-done.everyone, f32[256,1024]{1,0:T(8,128)S(1)} %prepare.1.scaled_ref), custom_call_target="tpu_custom_call" | custom-call | tf_op jit(solution)/shard_map/finish/pallas_call | solution.py:308
  (9 shorter events, 0.2 us)
Async XLA Ops:
  1.5 7.8 %collective-permute-start.1 = (bf16[1,2,256,128]{3,2,1,0:T(8,128)(2,1)S(1)}, bf16[1,2,256,128]{3,2,1,0:T(8,128)(2,1)S(1)}, u32[]{:S(2)}, u32[]{:S(2)}) collective-permute-start(bf16[1,2,256,128]{3,2,1,0:T(8,128)(2,1)S(1)} %maximum_bitcast_fusion.refs_3_), channel_id=1, source_target_pairs={{0,128},{8,136},{16,144},{24,152},{32,160},{40,168},{48,176},{56,1... | collective-permute-start | bytes 393224 | tf_op jit(solution)/shard_map/ppermute | solution.py:39
  2.8 6.5 %collective-permute-start = (bf16[1,2,256,128]{3,2,1,0:T(8,128)(2,1)S(1)}, bf16[1,2,256,128]{3,2,1,0:T(8,128)(2,1)S(1)}, u32[]{:S(2)}, u32[]{:S(2)}) collective-permute-start(bf16[1,2,256,128]{3,2,1,0:T(8,128)(2,1)S(1)} %maximum_bitcast_fusion.refs_3_), channel_id=1, source_target_pairs={{0,64},{8,72},{16,80},{24,88},{32,96},{40,104},{48,112},{56,120},{... | collective-permute-start | bytes 393224 | tf_op jit(solution)/shard_map/ppermute | solution.py:39
  9.4 9.8 %collective-permute-start.5 = (bf16[2,2,256,128]{3,2,1,0:T(8,128)(2,1)S(1)}, bf16[2,2,256,128]{3,2,1,0:T(8,128)(2,1)S(1)}, u32[]{:S(2)}, u32[]{:S(2)}) collective-permute-start(bf16[2,2,256,128]{3,2,1,0:T(8,128)(2,1)S(1)} %get-tuple-element.48), channel_id=1, source_target_pairs={{0,16},{8,24},{16,0},{24,8},{32,48},{40,56},{48,32},{56,40},{64,80... | collective-permute-start | bytes 786440 | tf_op jit(solution)/shard_map/ppermute | solution.py:39
  11.5 15.2 %collective-permute-start.2 = (bf16[2,2,256,128]{3,2,1,0:T(8,128)(2,1)S(1)}, bf16[2,2,256,128]{3,2,1,0:T(8,128)(2,1)S(1)}, u32[]{:S(2)}, u32[]{:S(2)}) collective-permute-start(bf16[2,2,256,128]{3,2,1,0:T(8,128)(2,1)S(1)} %get-tuple-element.49), channel_id=1, source_target_pairs={{0,32},{8,40},{16,48},{24,56},{32,0},{40,8},{48,16},{56,24},{64,96... | collective-permute-start | bytes 786440 | tf_op jit(solution)/shard_map/ppermute | solution.py:39
  13.5 19.1 %copy-start.1 = (bf16[1,256,1024]{2,1,0:T(8,128)(2,1)S(1)}, bf16[1,256,1024]{2,1,0:T(8,128)(2,1)}, u32[]{:S(2)}) copy-start(bf16[1,256,1024]{2,1,0:T(8,128)(2,1)} %param.6) | copy-start | bytes 1572868
  13.5 19.0 %copy-start.2 = (s32[8192]{0:T(1024)S(1)}, s32[8192]{0:T(1024)}, u32[]{:S(2)}) copy-start(s32[8192]{0:T(1024)} %param.9) | copy-start | bytes 98308
  13.5 29.6 %collective-permute-start.7 = (bf16[3,2,256,128]{3,2,1,0:T(8,128)(2,1)S(1)}, bf16[3,2,256,128]{3,2,1,0:T(8,128)(2,1)S(1)}, u32[]{:S(2)}, u32[]{:S(2)}) collective-permute-start(bf16[3,2,256,128]{3,2,1,0:T(8,128)(2,1)S(1)} %pad_maximum_fusion.1.refs_2_), channel_id=1, source_target_pairs={{0,8},{8,0},{16,24},{24,16},{32,40},{40,32},{48,56},{56,48},{64,72... | collective-permute-start | bytes 1179656 | tf_op jit(solution)/shard_map/ppermute | solution.py:39
  26.7 25.4 %collective-permute-start.6 = (bf16[4,2,256,128]{3,2,1,0:T(8,128)(2,1)S(1)}, bf16[4,2,256,128]{3,2,1,0:T(8,128)(2,1)S(1)}, u32[]{:S(2)}, u32[]{:S(2)}) collective-permute-start(bf16[4,2,256,128]{3,2,1,0:T(8,128)(2,1)S(1)} %pad_maximum_fusion), channel_id=1, source_target_pairs={{0,8},{8,0},{16,24},{24,16},{32,40},{40,32},{48,56},{56,48},{64,72... | collective-permute-start | bytes 1572872 | tf_op jit(solution)/shard_map/ppermute | solution.py:39
  30.6 9.7 %collective-permute-start.3 = (bf16[2,2,256,128]{3,2,1,0:T(8,128)(2,1)S(1)}, bf16[2,2,256,128]{3,2,1,0:T(8,128)(2,1)S(1)}, u32[]{:S(2)}, u32[]{:S(2)}) collective-permute-start(bf16[2,2,256,128]{3,2,1,0:T(8,128)(2,1)S(1)} %collective-permute-done.2.refs_2_), channel_id=1, source_target_pairs={{0,16},{8,24},{16,0},{24,8},{32,48},{40,56},{48,32},{56,40},{64,80... | collective-permute-start | bytes 786440 | tf_op jit(solution)/shard_map/ppermute | solution.py:39
  40.4 19.2 %collective-permute-start.4 = (bf16[2,2,256,128]{3,2,1,0:T(8,128)(2,1)S(1)}, bf16[2,2,256,128]{3,2,1,0:T(8,128)(2,1)S(1)}, u32[]{:S(2)}, u32[]{:S(2)}) collective-permute-start(bf16[2,2,256,128]{3,2,1,0:T(8,128)(2,1)S(1)} %collective-permute-done.3.refs_2_), channel_id=1, source_target_pairs={{0,8},{8,0},{16,24},{24,16},{32,40},{40,32},{48,56},{56,48},{64,72... | collective-permute-start | bytes 786440 | tf_op jit(solution)/shard_map/ppermute | solution.py:39
  56.9 2.7 %copy-start.3 = (f32[1,1024]{1,0:T(1,128)S(1)}, f32[1,1024]{1,0:T(1,128)}, u32[]{:S(2)}) copy-start(f32[1,1024]{1,0:T(1,128)} %refs_7_.1) | copy-start | bytes 12292
  59.5 0.7 copy-start
  64.0 24.9 %all-to-all-start = ((f32[16,1,512]{2,1,0:T(1,128)}), f32[16,1,512]{2,1,0:T(1,128)S(1)}, u32[]{:S(2)}, u32[]{:S(2)}) async-start(f32[16,1,512]{2,1,0:T(1,128)} %get-tuple-element.44), calls=%async_computation | async-start | bytes 65536 | tf_op jit(solution)/shard_map/all_to_all | solution.py:299
where the time goes:
time: 90.3 us; the launch traced here: 89.8 us
  starting transfers between devices  32.9 us (36%)
  waiting for transfers between devices  31.2 us (35%)
  Pallas kernels  23.1 us (26%)
  other arithmetic  1.03 us (1%)
    pallas_call x7, Pallas kernels, attend(): pl.pallas_call(functools.partial(attend_kernel, plan, first, last, member...  21.9 us
    ppermute x8, waiting for transfers between devices, moved(): return lax.ppermute(block, 'ctx', route)  20.1 us
    ppermute x8, starting transfers between devices, moved(): return lax.ppermute(block, 'ctx', route)  19.3 us
    all_to_all x1, starting transfers between devices, local(): everyone = lax.all_to_all(stats, ('branch', 'tp'), 0, 0, tiled=True)  13.6 us
    all_to_all x1, waiting for transfers between devices, local(): everyone = lax.all_to_all(stats, ('branch', 'tp'), 0, 0, tiled=True)  11.1 us
  transfers between devices with their start and end apart: 9, of which 5 were waited for; matrix products, arithmetic and copies ran while one was open for 0% of the time, Pallas kernels for 20%

commit v1 on v0

--- a/solution.py
+++ b/solution.py
@@ -41,8 +41,8 @@
 
 def attend_kernel(plan, first, last, members, *refs):
     if first:
-        here_ref, segments_ref, q_ref = refs[:3]
-        refs = refs[3:]
+        here_ref, branch_ref, gain_ref, weight_ref, segments_ref, q_ref = refs[:6]
+        refs = refs[6:]
     else:
         meta_ref, q_ref = refs[:2]
         refs = refs[2:]
@@ -51,10 +51,10 @@
         m_in, l_in, acc_in = refs[:3]
         refs = refs[3:]
     if last:
-        gain_ref, weight_ref = refs[:2]
-        att_ref, stats_ref, m_ref, l_ref, acc_ref = refs[2:]
+        gain_ref, pieces_ref = refs[:2]
+        scaled_ref, stats_ref, m_ref, l_ref, acc_ref = refs[2:]
     elif first:
-        meta_ref, m_ref, l_ref, acc_ref = refs
+        meta_ref, held_gain_ref, pieces_ref, m_ref, l_ref, acc_ref = refs
     else:
         m_ref, l_ref, acc_ref = refs
     rows = q_ref.shape[0]
@@ -66,6 +66,16 @@
         here = here_ref[0]
         segments = segments_ref[...]
         meta_ref[0] = here
+        meta_ref[4] = branch_ref[0]
+        gain = gain_ref[...]
+        held_gain_ref[...] = gain
+        rest = gain * weight_ref[...]
+        pieces = []
+        for _ in range(3):
+            pieces.append(rest.astype(jnp.bfloat16).astype(jnp.float32))
+            rest = rest - pieces[-1]
+        pieces.append(jnp.zeros((5, rest.shape[1]), jnp.float32))
+        pieces_ref[...] = jnp.concatenate(pieces, axis=0).astype(jnp.bfloat16)
         bounds = []
         for s in (1, 2, 3):
             ahead = jnp.sum((segments < s).astype(jnp.float32)).astype(jnp.int32)
@@ -167,23 +177,15 @@
     if last:
         squares = jnp.zeros((8, rows), jnp.float32)
         dotted = jnp.zeros((8, rows), jnp.float32)
-        product = gain_ref[...] * weight_ref[...]
-        pieces = []
-        for _ in range(3):
-            pieces.append(product.astype(jnp.bfloat16))
-            product = product - pieces[-1].astype(jnp.float32)
-        pieces = jnp.concatenate(
-            [p.astype(jnp.float32) for p in pieces] + [jnp.zeros((5, product.shape[1]), jnp.float32)],
-            axis=0,
-        ).astype(jnp.bfloat16)
         for g in range(heads):
             part = acc_ref[g].reshape(HD // 8, 8, rows) / l_ref[g][None]
             attended = part.reshape(HD, rows).astype(jnp.bfloat16)
-            att_ref[g] = attended
             wide = attended.astype(jnp.float32)
+            at = slice(g * HD, (g + 1) * HD)
+            scaled_ref[:, at] = wide.T * gain_ref[:, at]
             squares += jnp.sum((wide * wide).reshape(HD // 8, 8, rows), axis=0)
             dotted += jnp.dot(
-                pieces[:, g * HD : (g + 1) * HD], attended, preferred_element_type=jnp.float32
+                pieces_ref[:, at], attended, preferred_element_type=jnp.float32
             )
         line = jnp.concatenate(
             [jnp.sum(v, axis=0, keepdims=True) for v in (squares, dotted)], axis=1
@@ -202,9 +204,10 @@
     state_shapes = [(heads, 8, rows), (heads, 8, rows), (heads, HD, rows)]
     operands = [*operands, *blocks, *(state or ()), *(gains or ())]
     scratch = []
+    scalars = 2 if first else 1
     if last:
         out_shape = (
-            jax.ShapeDtypeStruct((heads, HD, rows), jnp.bfloat16),
+            jax.ShapeDtypeStruct((rows, width), jnp.float32),
             jax.ShapeDtypeStruct((members, 1, 2 * rows), jnp.float32),
         )
         out_specs = (VMEM, VMEM)
@@ -213,13 +216,17 @@
         out_shape = tuple(jax.ShapeDtypeStruct(s, jnp.float32) for s in state_shapes)
         out_specs = (VMEM,) * 3
         if first:
-            out_shape = (jax.ShapeDtypeStruct((4,), jnp.int32),) + out_shape
-            out_specs = (SMEM,) + out_specs
+            out_shape = (
+                jax.ShapeDtypeStruct((5,), jnp.int32),
+                jax.ShapeDtypeStruct((1, width), jnp.float32),
+                jax.ShapeDtypeStruct((8, width), jnp.bfloat16),
+            ) + out_shape
+            out_specs = (SMEM, VMEM, VMEM) + out_specs
     pairs = sum(p[0] for p in plan) * blocks[0].shape[2] * rows * heads
     return pl.pallas_call(
         functools.partial(attend_kernel, plan, first, last, members),
         out_shape=out_shape,
-        in_specs=[SMEM] + [VMEM] * (len(operands) - 1),
+        in_specs=[SMEM] * scalars + [VMEM] * (len(operands) - scalars),
         out_specs=out_specs,
         scratch_shapes=scratch,
         compiler_params=SMALL,
@@ -230,17 +237,10 @@
     )(*operands)
 
 
-def prepare_kernel(att_ref, gain_ref, out_ref):
-    heads = att_ref.shape[0]
-    for g in range(heads):
-        at = slice(g * HD, (g + 1) * HD)
-        out_ref[:, at] = att_ref[g].astype(jnp.float32).T * gain_ref[:, at]
-
-
-def finish_kernel(branches, mine_ref, everyone, scaled_ref, normed_ref, joined_ref):
+def finish_kernel(branches, meta_ref, everyone, scaled_ref, normed_ref, joined_ref):
     rows, width = scaled_ref.shape
     size = everyone.shape[0] // branches
-    mine = mine_ref[0]
+    mine = meta_ref[4]
     joined = jnp.zeros((1, rows), jnp.float32)
     own = jnp.zeros((1, rows), jnp.float32)
     for b in range(branches):
@@ -269,8 +269,17 @@
     from_1 = moved(own, lambda x, y, c: (x + 1, y, c))
     from_2 = moved(own, lambda x, y, c: (x + 2, y, c))
 
-    meta, *state = attend(
-        [here.reshape(1), segments.reshape(-1, HD), q], [own], ((1, 0, 0, 0),)
+    meta, gain, pieces, *state = attend(
+        [
+            here.reshape(1),
+            lax.axis_index("branch").reshape(1),
+            norm_gain,
+            head_weight,
+            segments.reshape(-1, HD),
+            q,
+        ],
+        [own],
+        ((1, 0, 0, 0),),
     )
     column = jnp.concatenate([from_2, from_1, own])
     pick = lambda up: jnp.where(up, column[1:], column[:2])
@@ -288,23 +297,10 @@
     state = attend([meta, q], [across_3], ((2, None, 3, 0),), state)
     branches = lax.axis_size("branch")
     members = branches * lax.axis_size("tp")
-    attended, stats = attend(
-        [meta, q],
-        [across_3p],
-        ((2, None, 3, 1),),
-        state,
-        (norm_gain, head_weight),
-        members,
+    scaled, stats = attend(
+        [meta, q], [across_3p], ((2, None, 3, 1),), state, (gain, pieces), members
     )
     everyone = lax.all_to_all(stats, ("branch", "tp"), 0, 0, tiled=True)
-    scaled = pl.pallas_call(
-        prepare_kernel,
-        out_shape=jax.ShapeDtypeStruct((rows, width), jnp.float32),
-        in_specs=[VMEM] * 2,
-        out_specs=VMEM,
-        compiler_params=SMALL,
-        name="prepare",
-    )(attended, norm_gain)
     normed, joined = pl.pallas_call(
         functools.partial(finish_kernel, branches),
         out_shape=(
@@ -315,7 +311,7 @@
         out_specs=(VMEM,) * 2,
         compiler_params=SMALL,
         name="finish",
-    )(lax.axis_index("branch").reshape(1), everyone, scaled)
+    )(meta, everyone, scaled)
     return (normed[None], joined[0])
 
 

time: 90.3 us -> 89.2 us (0.988)
  blocking collectives: 0 us -> 24.7 us
  starting transfers between devices: 32.9 us -> 19.3 us
  waiting for transfers between devices: 31.2 us -> 19.4 us
    all_to_all x0 -> x1, blocking collectives: none -> 24.7 us  [local(): everyone = lax.all_to_all(stats, ('branch', 'tp'), 0, 0, tiled=True)]
    all_to_all x1 -> x0, starting transfers between devices: 13.6 us -> none  [local(): everyone = lax.all_to_all(stats, ('branch', 'tp'), 0, 0, tiled=True)]
    all_to_all x1 -> x0, waiting for transfers between devices: 11.1 us -> none  [local(): everyone = lax.all_to_all(stats, ('branch', 'tp'), 0, 0, tiled=True)]
  transfers between devices with their start and end apart: 9 -> 8, of which waited for: 5 -> 4; matrix products, arithmetic and copies ran while one was open for 0% -> 0% of each run, Pallas kernels for 20% -> 20%
where the time goes in v1:
time: 89.2 us; the launch traced here: 88.8 us
  blocking collectives  24.7 us (28%)
  Pallas kernels  22.7 us (25%)
  waiting for transfers between devices  19.4 us (22%)
  starting transfers between devices  19.3 us (22%)
  other arithmetic  1.03 us (1%)
    all_to_all x1, blocking collectives, local(): everyone = lax.all_to_all(stats, ('branch', 'tp'), 0, 0, tiled=True)  24.7 us
    pallas_call x7, Pallas kernels, attend(): pl.pallas_call(functools.partial(attend_kernel, plan, first, last, member...  21.2 us
    ppermute x8, waiting for transfers between devices, moved(): return lax.ppermute(block, 'ctx', route)  19.4 us
    ppermute x8, starting transfers between devices, moved(): return lax.ppermute(block, 'ctx', route)  19.3 us
  transfers between devices with their start and end apart: 8, of which 4 were waited for; matrix products, arithmetic and copies ran while one was open for 0% of the time, Pallas kernels for 20%

profile of v1, /device:TPU:31, one launch (start us, length us, event | category | flops | bytes accessed | tf_op | source)
XLA Modules:
  0.0 88.8 jit_solution(2987819660610138666)
XLA Ops:
  0.6 0.9 maximum_bitcast_fusion.refs_6_
  1.5 1.3 %collective-permute-start.1 = (bf16[1,2,256,128]{3,2,1,0:T(8,128)(2,1)S(1)}, bf16[1,2,256,128]{3,2,1,0:T(8,128)(2,1)S(1)}, u32[]{:S(2)}, u32[]{:S(2)}) collective-permute-start(bf16[1,2,256,128]{3,2,1,0:T(8,128)(2,1)S(1)} %maximum_bitcast_fusion.refs_6_), channel_id=1, source_target_pairs={{0,128},{8,136},{16,144},{24,152},{32,160},{40,168},{48,176},{56,1... | collective-permute-start | bytes 393224 | tf_op jit(solution)/shard_map/ppermute | solution.py:39
  2.8 1.3 %collective-permute-start = (bf16[1,2,256,128]{3,2,1,0:T(8,128)(2,1)S(1)}, bf16[1,2,256,128]{3,2,1,0:T(8,128)(2,1)S(1)}, u32[]{:S(2)}, u32[]{:S(2)}) collective-permute-start(bf16[1,2,256,128]{3,2,1,0:T(8,128)(2,1)S(1)} %maximum_bitcast_fusion.refs_6_), channel_id=1, source_target_pairs={{0,64},{8,72},{16,80},{24,88},{32,96},{40,104},{48,112},{56,120},{... | collective-permute-start | bytes 393224 | tf_op jit(solution)/shard_map/ppermute | solution.py:39
  4.1 5.2 %collective-permute-done.1 = bf16[1,2,256,128]{3,2,1,0:T(8,128)(2,1)S(1)} collective-permute-done((bf16[1,2,256,128]{3,2,1,0:T(8,128)(2,1)S(1)}, bf16[1,2,256,128]{3,2,1,0:T(8,128)(2,1)S(1)}, u32[]{:S(2)}, u32[]{:S(2)}) %collective-permute-start.1) | collective-permute-done | bytes 131104 | tf_op jit(solution)/shard_map/ppermute | solution.py:39
  9.3 0.0 collective-permute-done
  9.4 2.1 %collective-permute-start.5 = (bf16[2,2,256,128]{3,2,1,0:T(8,128)(2,1)S(1)}, bf16[2,2,256,128]{3,2,1,0:T(8,128)(2,1)S(1)}, u32[]{:S(2)}, u32[]{:S(2)}) collective-permute-start(bf16[2,2,256,128]{3,2,1,0:T(8,128)(2,1)S(1)} %get-tuple-element.52), channel_id=1, source_target_pairs={{0,16},{8,24},{16,0},{24,8},{32,48},{40,56},{48,32},{56,40},{64,80... | collective-permute-start | bytes 786440 | tf_op jit(solution)/shard_map/ppermute | solution.py:39
  11.5 2.0 %collective-permute-start.2 = (bf16[2,2,256,128]{3,2,1,0:T(8,128)(2,1)S(1)}, bf16[2,2,256,128]{3,2,1,0:T(8,128)(2,1)S(1)}, u32[]{:S(2)}, u32[]{:S(2)}) collective-permute-start(bf16[2,2,256,128]{3,2,1,0:T(8,128)(2,1)S(1)} %get-tuple-element.53), channel_id=1, source_target_pairs={{0,32},{8,40},{16,48},{24,56},{32,0},{40,8},{48,16},{56,24},{64,96... | collective-permute-start | bytes 786440 | tf_op jit(solution)/shard_map/ppermute | solution.py:39
  13.5 0.0 copy-start
  13.5 0.0 copy-start.1
  13.5 4.1 %collective-permute-start.7 = (bf16[3,2,256,128]{3,2,1,0:T(8,128)(2,1)S(1)}, bf16[3,2,256,128]{3,2,1,0:T(8,128)(2,1)S(1)}, u32[]{:S(2)}, u32[]{:S(2)}) collective-permute-start(bf16[3,2,256,128]{3,2,1,0:T(8,128)(2,1)S(1)} %pad_maximum_fusion.1.refs_2_), channel_id=1, source_target_pairs={{0,8},{8,0},{16,24},{24,16},{32,40},{40,32},{48,56},{56,48},{64,72... | collective-permute-start | bytes 1179656 | tf_op jit(solution)/shard_map/ppermute | solution.py:39
  17.7 1.5 %collective-permute-done.5.refs_2_ = bf16[2,2,256,128]{3,2,1,0:T(8,128)(2,1)S(1)} collective-permute-done((bf16[2,2,256,128]{3,2,1,0:T(8,128)(2,1)S(1)}, bf16[2,2,256,128]{3,2,1,0:T(8,128)(2,1)S(1)}, u32[]{:S(2)}, u32[]{:S(2)}) %collective-permute-start.5) | collective-permute-done | bytes 262176 | tf_op jit(solution)/shard_map/ppermute | solution.py:39
  19.2 7.5 %collective-permute-done.2.refs_2_ = bf16[2,2,256,128]{3,2,1,0:T(8,128)(2,1)S(1)} collective-permute-done((bf16[2,2,256,128]{3,2,1,0:T(8,128)(2,1)S(1)}, bf16[2,2,256,128]{3,2,1,0:T(8,128)(2,1)S(1)}, u32[]{:S(2)}, u32[]{:S(2)}) %collective-permute-start.2) | collective-permute-done | bytes 262176 | tf_op jit(solution)/shard_map/ppermute | solution.py:39
  26.7 3.9 %collective-permute-start.6 = (bf16[4,2,256,128]{3,2,1,0:T(8,128)(2,1)S(1)}, bf16[4,2,256,128]{3,2,1,0:T(8,128)(2,1)S(1)}, u32[]{:S(2)}, u32[]{:S(2)}) collective-permute-start(bf16[4,2,256,128]{3,2,1,0:T(8,128)(2,1)S(1)} %pad_maximum_fusion), channel_id=1, source_target_pairs={{0,8},{8,0},{16,24},{24,16},{32,40},{40,32},{48,56},{56,48},{64,72... | collective-permute-start | bytes 1572872 | tf_op jit(solution)/shard_map/ppermute | solution.py:39
  30.6 1.9 %collective-permute-start.3 = (bf16[2,2,256,128]{3,2,1,0:T(8,128)(2,1)S(1)}, bf16[2,2,256,128]{3,2,1,0:T(8,128)(2,1)S(1)}, u32[]{:S(2)}, u32[]{:S(2)}) collective-permute-start(bf16[2,2,256,128]{3,2,1,0:T(8,128)(2,1)S(1)} %collective-permute-done.2.refs_2_), channel_id=1, source_target_pairs={{0,16},{8,24},{16,0},{24,8},{32,48},{40,56},{48,32},{56,40},{64,80... | collective-permute-start | bytes 786440 | tf_op jit(solution)/shard_map/ppermute | solution.py:39
  32.6 0.0 copy-start.3
  32.6 0.0 copy-start.2
  32.6 0.6 copy-done.3
  33.3 0.0 copy-done.2
  33.3 1.9 %attend.7 = (s32[5]{0:T(128)S(1)}, f32[1,1024]{1,0:T(1,128)S(1)}, bf16[8,1024]{1,0:T(8,128)(2,1)S(1)}, f32[8,8,256]{2,1,0:T(8,128)S(1)}, f32[8,8,256]{2,1,0:T(8,128)S(1)}, /*index=5*/f32[8,128,256]{2,1,0:T(8,128)S(1)}) custom-call(s32[1]{0:T(128)} %bitcast.refs_0_, s32[1]{0:T(128)} %bitcast.1.refs_1_, f32[1,1024]{1,0:T(1,128)S(1)} %copy-done.2, ...), custom_call_target="tpu_custom_call" | custom-call | flops 268435456 | bytes 1048576 | tf_op jit(solution)/shard_map/attend/pallas_call | solution.py:226
  35.2 5.2 %collective-permute-done.3.refs_2_ = bf16[2,2,256,128]{3,2,1,0:T(8,128)(2,1)S(1)} collective-permute-done((bf16[2,2,256,128]{3,2,1,0:T(8,128)(2,1)S(1)}, bf16[2,2,256,128]{3,2,1,0:T(8,128)(2,1)S(1)}, u32[]{:S(2)}, u32[]{:S(2)}) %collective-permute-start.3) | collective-permute-done | bytes 262176 | tf_op jit(solution)/shard_map/ppermute | solution.py:39
  40.4 2.8 %collective-permute-start.4 = (bf16[2,2,256,128]{3,2,1,0:T(8,128)(2,1)S(1)}, bf16[2,2,256,128]{3,2,1,0:T(8,128)(2,1)S(1)}, u32[]{:S(2)}, u32[]{:S(2)}) collective-permute-start(bf16[2,2,256,128]{3,2,1,0:T(8,128)(2,1)S(1)} %collective-permute-done.3.refs_2_), channel_id=1, source_target_pairs={{0,8},{8,0},{16,24},{24,16},{32,40},{40,32},{48,56},{56,48},{64,72... | collective-permute-start | bytes 786440 | tf_op jit(solution)/shard_map/ppermute | solution.py:39
  43.2 0.0 collective-permute-done.7.refs_3_
  43.2 3.7 %attend.8 = (f32[8,8,256]{2,1,0:T(8,128)S(1)}, f32[8,8,256]{2,1,0:T(8,128)S(1)}, f32[8,128,256]{2,1,0:T(8,128)S(1)}) custom-call(s32[5]{0:T(128)S(1)} %get-tuple-element.27.refs_0_.meta_ref, bf16[256,1024]{1,0:T(8,128)(2,1)S(1)} %bitcast.9, bf16[3,2,256,128]{3,2,1,0:T(8,128)(2,1)S(1)} %pad_maximum_fusion.1.refs_2_, ...), custom_call_target="tpu_custom_call" | custom-call | flops 1342177280 | bytes 1048576 | tf_op jit(solution)/shard_map/attend/pallas_call | solution.py:226
  46.9 2.6 %attend.9 = (f32[8,8,256]{2,1,0:T(8,128)S(1)}, f32[8,8,256]{2,1,0:T(8,128)S(1)}, f32[8,128,256]{2,1,0:T(8,128)S(1)}) custom-call(s32[5]{0:T(128)S(1)} %get-tuple-element.27.refs_0_.meta_ref, bf16[256,1024]{1,0:T(8,128)(2,1)S(1)} %bitcast.10, bf16[2,2,256,128]{3,2,1,0:T(8,128)(2,1)S(1)} %collective-permute-done.5.refs_2_, ...), custom_call_target="tpu_custom_call" | custom-call | flops 536870912 | bytes 1048576 | tf_op jit(solution)/shard_map/attend/pallas_call | solution.py:226
  49.5 2.6 %attend.10 = (f32[8,8,256]{2,1,0:T(8,128)S(1)}, f32[8,8,256]{2,1,0:T(8,128)S(1)}, f32[8,128,256]{2,1,0:T(8,128)S(1)}) custom-call(s32[5]{0:T(128)S(1)} %get-tuple-element.27.refs_0_.meta_ref, bf16[256,1024]{1,0:T(8,128)(2,1)S(1)} %bitcast.11, bf16[2,2,256,128]{3,2,1,0:T(8,128)(2,1)S(1)} %collective-permute-done.2.refs_2_, ...), custom_call_target="tpu_custom_call" | custom-call | flops 536870912 | bytes 1048576 | tf_op jit(solution)/shard_map/attend/pallas_call | solution.py:226
  52.2 0.0 collective-permute-done.6.refs_2_
  52.2 4.7 %attend.11 = (f32[8,8,256]{2,1,0:T(8,128)S(1)}, f32[8,8,256]{2,1,0:T(8,128)S(1)}, f32[8,128,256]{2,1,0:T(8,128)S(1)}) custom-call(s32[5]{0:T(128)S(1)} %get-tuple-element.27.refs_0_.meta_ref, bf16[256,1024]{1,0:T(8,128)(2,1)S(1)} %bitcast.12, bf16[4,2,256,128]{3,2,1,0:T(8,128)(2,1)S(1)} %collective-permute-done.6.refs_2_, ...), custom_call_target="tpu_custom_call" | custom-call | flops 1073741824 | bytes 1048576 | tf_op jit(solution)/shard_map/attend/pallas_call | solution.py:226
  56.9 2.6 %attend.12 = (f32[8,8,256]{2,1,0:T(8,128)S(1)}, f32[8,8,256]{2,1,0:T(8,128)S(1)}, f32[8,128,256]{2,1,0:T(8,128)S(1)}) custom-call(s32[5]{0:T(128)S(1)} %get-tuple-element.27.refs_0_.meta_ref, bf16[256,1024]{1,0:T(8,128)(2,1)S(1)} %bitcast.13, bf16[2,2,256,128]{3,2,1,0:T(8,128)(2,1)S(1)} %collective-permute-done.3.refs_2_, ...), custom_call_target="tpu_custom_call" | custom-call | flops 536870912 | bytes 1048576 | tf_op jit(solution)/shard_map/attend/pallas_call | solution.py:226
  59.5 0.0 collective-permute-done.4.refs_2_
  59.5 3.1 %attend.13 = (f32[256,1024]{1,0:T(8,128)S(1)}, f32[16,1,512]{2,1,0:T(1,128)S(1)}) custom-call(s32[5]{0:T(128)S(1)} %get-tuple-element.27.refs_0_.meta_ref, bf16[256,1024]{1,0:T(8,128)(2,1)S(1)} %bitcast.14, bf16[2,2,256,128]{3,2,1,0:T(8,128)(2,1)S(1)} %collective-permute-done.4.refs_2_, f32[8,8,256]{2,1,0:T(8,128)S(1)} %get-tuple-element.43.refs_3_, ...), custom_call_target="tpu_custom_call" | custom-call | flops 536870912 | bytes 1048576 | tf_op jit(solution)/shard_map/attend/pallas_call | solution.py:226
  62.6 24.7 %all_to_all.5.everyone = f32[16,1,512]{2,1,0:T(1,128)S(1)} all-to-all(f32[16,1,512]{2,1,0:T(1,128)S(1)} %get-tuple-element.48), channel_id=1, replica_groups=mesh['branch'=2,'ctx'=32,'tp'=8] {'branch','tp'}, dimensions={0} | all-to-all | bytes 65536 | tf_op jit(solution)/shard_map/all_to_all | solution.py:303
  87.3 1.5 %finish.1 = (bf16[256,1024]{1,0:T(8,128)(2,1)}, f32[1,256]{1,0:T(1,128)}) custom-call(s32[5]{0:T(128)S(1)} %get-tuple-element.27.refs_0_.meta_ref, f32[16,1,512]{2,1,0:T(1,128)S(1)} %all_to_all.5.everyone, f32[256,1024]{1,0:T(8,128)S(1)} %get-tuple-element.49.scaled_ref), custom_call_target="tpu_custom_call" | custom-call | tf_op jit(solution)/shard_map/finish/pallas_call | solution.py:304
  (7 shorter events, 0.2 us)
Async XLA Ops:
  1.5 7.8 %collective-permute-start.1 = (bf16[1,2,256,128]{3,2,1,0:T(8,128)(2,1)S(1)}, bf16[1,2,256,128]{3,2,1,0:T(8,128)(2,1)S(1)}, u32[]{:S(2)}, u32[]{:S(2)}) collective-permute-start(bf16[1,2,256,128]{3,2,1,0:T(8,128)(2,1)S(1)} %maximum_bitcast_fusion.refs_6_), channel_id=1, source_target_pairs={{0,128},{8,136},{16,144},{24,152},{32,160},{40,168},{48,176},{56,1... | collective-permute-start | bytes 393224 | tf_op jit(solution)/shard_map/ppermute | solution.py:39
  2.8 6.5 %collective-permute-start = (bf16[1,2,256,128]{3,2,1,0:T(8,128)(2,1)S(1)}, bf16[1,2,256,128]{3,2,1,0:T(8,128)(2,1)S(1)}, u32[]{:S(2)}, u32[]{:S(2)}) collective-permute-start(bf16[1,2,256,128]{3,2,1,0:T(8,128)(2,1)S(1)} %maximum_bitcast_fusion.refs_6_), channel_id=1, source_target_pairs={{0,64},{8,72},{16,80},{24,88},{32,96},{40,104},{48,112},{56,120},{... | collective-permute-start | bytes 393224 | tf_op jit(solution)/shard_map/ppermute | solution.py:39
  9.4 9.8 %collective-permute-start.5 = (bf16[2,2,256,128]{3,2,1,0:T(8,128)(2,1)S(1)}, bf16[2,2,256,128]{3,2,1,0:T(8,128)(2,1)S(1)}, u32[]{:S(2)}, u32[]{:S(2)}) collective-permute-start(bf16[2,2,256,128]{3,2,1,0:T(8,128)(2,1)S(1)} %get-tuple-element.52), channel_id=1, source_target_pairs={{0,16},{8,24},{16,0},{24,8},{32,48},{40,56},{48,32},{56,40},{64,80... | collective-permute-start | bytes 786440 | tf_op jit(solution)/shard_map/ppermute | solution.py:39
  11.5 15.2 %collective-permute-start.2 = (bf16[2,2,256,128]{3,2,1,0:T(8,128)(2,1)S(1)}, bf16[2,2,256,128]{3,2,1,0:T(8,128)(2,1)S(1)}, u32[]{:S(2)}, u32[]{:S(2)}) collective-permute-start(bf16[2,2,256,128]{3,2,1,0:T(8,128)(2,1)S(1)} %get-tuple-element.53), channel_id=1, source_target_pairs={{0,32},{8,40},{16,48},{24,56},{32,0},{40,8},{48,16},{56,24},{64,96... | collective-permute-start | bytes 786440 | tf_op jit(solution)/shard_map/ppermute | solution.py:39
  13.5 19.1 %copy-start = (bf16[1,256,1024]{2,1,0:T(8,128)(2,1)S(1)}, bf16[1,256,1024]{2,1,0:T(8,128)(2,1)}, u32[]{:S(2)}) copy-start(bf16[1,256,1024]{2,1,0:T(8,128)(2,1)} %param.6) | copy-start | bytes 1572868
  13.5 19.1 %copy-start.1 = (s32[8192]{0:T(1024)S(1)}, s32[8192]{0:T(1024)}, u32[]{:S(2)}) copy-start(s32[8192]{0:T(1024)} %param.9) | copy-start | bytes 98308
  13.5 29.6 %collective-permute-start.7 = (bf16[3,2,256,128]{3,2,1,0:T(8,128)(2,1)S(1)}, bf16[3,2,256,128]{3,2,1,0:T(8,128)(2,1)S(1)}, u32[]{:S(2)}, u32[]{:S(2)}) collective-permute-start(bf16[3,2,256,128]{3,2,1,0:T(8,128)(2,1)S(1)} %pad_maximum_fusion.1.refs_2_), channel_id=1, source_target_pairs={{0,8},{8,0},{16,24},{24,16},{32,40},{40,32},{48,56},{56,48},{64,72... | collective-permute-start | bytes 1179656 | tf_op jit(solution)/shard_map/ppermute | solution.py:39
  26.7 25.4 %collective-permute-start.6 = (bf16[4,2,256,128]{3,2,1,0:T(8,128)(2,1)S(1)}, bf16[4,2,256,128]{3,2,1,0:T(8,128)(2,1)S(1)}, u32[]{:S(2)}, u32[]{:S(2)}) collective-permute-start(bf16[4,2,256,128]{3,2,1,0:T(8,128)(2,1)S(1)} %pad_maximum_fusion), channel_id=1, source_target_pairs={{0,8},{8,0},{16,24},{24,16},{32,40},{40,32},{48,56},{56,48},{64,72... | collective-permute-start | bytes 1572872 | tf_op jit(solution)/shard_map/ppermute | solution.py:39
  30.6 9.7 %collective-permute-start.3 = (bf16[2,2,256,128]{3,2,1,0:T(8,128)(2,1)S(1)}, bf16[2,2,256,128]{3,2,1,0:T(8,128)(2,1)S(1)}, u32[]{:S(2)}, u32[]{:S(2)}) collective-permute-start(bf16[2,2,256,128]{3,2,1,0:T(8,128)(2,1)S(1)} %collective-permute-done.2.refs_2_), channel_id=1, source_target_pairs={{0,16},{8,24},{16,0},{24,8},{32,48},{40,56},{48,32},{56,40},{64,80... | collective-permute-start | bytes 786440 | tf_op jit(solution)/shard_map/ppermute | solution.py:39
  32.6 0.7 copy-start.3
  32.6 0.7 copy-start.2
  40.4 19.1 %collective-permute-start.4 = (bf16[2,2,256,128]{3,2,1,0:T(8,128)(2,1)S(1)}, bf16[2,2,256,128]{3,2,1,0:T(8,128)(2,1)S(1)}, u32[]{:S(2)}, u32[]{:S(2)}) collective-permute-start(bf16[2,2,256,128]{3,2,1,0:T(8,128)(2,1)S(1)} %collective-permute-done.3.refs_2_), channel_id=1, source_target_pairs={{0,8},{8,0},{16,24},{24,16},{32,40},{40,32},{48,56},{56,48},{64,72... | collective-permute-start | bytes 786440 | tf_op jit(solution)/shard_map/ppermute | solution.py:39

commit v2 on v1

--- a/solution.py
+++ b/solution.py
@@ -15,7 +15,7 @@
 EPSILON = 1e-06
 
 NX, NY = 4, 4
-AHEAD, BEHIND = 2, 1
+AHEAD, BEHIND = 3, 2
 
 
 VMEM = pl.BlockSpec(memory_space=pltpu.VMEM)
@@ -54,7 +54,7 @@
         gain_ref, pieces_ref = refs[:2]
         scaled_ref, stats_ref, m_ref, l_ref, acc_ref = refs[2:]
     elif first:
-        meta_ref, held_gain_ref, pieces_ref, m_ref, l_ref, acc_ref = refs
+        meta_ref, side_ref, held_gain_ref, pieces_ref, m_ref, l_ref, acc_ref = refs
     else:
         m_ref, l_ref, acc_ref = refs
     rows = q_ref.shape[0]
@@ -66,7 +66,7 @@
         here = here_ref[0]
         segments = segments_ref[...]
         meta_ref[0] = here
-        meta_ref[4] = branch_ref[0]
+        side_ref[...] = jnp.full(side_ref.shape, branch_ref[0], jnp.int32)
         gain = gain_ref[...]
         held_gain_ref[...] = gain
         rest = gain * weight_ref[...]
@@ -104,10 +104,14 @@
         l_ref[...] = l_in[...]
         acc_ref[...] = acc_in[...]
 
-    def visit(key_rows, value_rows, offset, masked):
+    def visit(kv_ref, entries, offsets, masked):
+        join = lambda n: jnp.concatenate([kv_ref[j, n] for j in entries], axis=0)
+        key_rows, value_rows = join(0), join(1)
+        keys = key_rows.shape[0]
         tall = jnp.concatenate([value_rows.T, jnp.ones((16, keys), jnp.bfloat16)], axis=0)
         if masked:
-            key_pos = offset + lax.broadcasted_iota(jnp.int32, (keys, rows), 0)
+            within = lax.broadcasted_iota(jnp.int32, (rows, rows), 0)
+            key_pos = jnp.concatenate([offset + within for offset in offsets], axis=0)
             query_pos = first_row + lax.broadcasted_iota(jnp.int32, (1, rows), 1)
             allowed = (key_pos >= start_of(query_pos)) & (key_pos <= query_pos)
 
@@ -148,8 +152,7 @@
 
     for kv_ref, (count, shift, across, flip) in zip(kv_refs, plan):
 
-        def one(i, carry, kv_ref=kv_ref, count=count, shift=shift, across=across, flip=flip):
-            j = count - 1 - i
+        def place(j, shift=shift, across=across, flip=flip):
             if shift is not None:
                 yy, xx = y, x + shift + j
             else:
@@ -159,20 +162,35 @@
             offset = (((xx * NY + yy) * 2) + jnp.bitwise_xor(core, flip)) * rows
             valid = (xx >= 0) & (offset <= first_row) & (offset + keys > low)
             clear = (offset >= high) & (offset + keys <= first_row)
+            return offset, valid, clear
+
+        def take(entries, kv_ref=kv_ref, place=place):
+            offsets, valids, clears = zip(*[place(j) for j in entries])
+            valid, clear = valids[0], valids[0] & clears[0]
+            for v, c in zip(valids[1:], clears[1:]):
+                valid, clear = valid | v, clear & v & c
 
             if not first:
 
-                @pl.when(valid & clear)
+                @pl.when(clear)
                 def _():
-                    visit(kv_ref[j, 0], kv_ref[j, 1], offset, False)
-
-            @pl.when(valid if first else valid & ~clear)
+                    visit(kv_ref, entries, offsets, False)
+
+            @pl.when(valid & ~clear)
             def _():
-                visit(kv_ref[j, 0], kv_ref[j, 1], offset, True)
-
-            return carry
-
-        lax.fori_loop(0, count, one, 0)
+                visit(kv_ref, entries, offsets, True)
+
+        if count == 2:
+            take([0, 1])
+        elif count > 1:
+
+            def pair(i, carry, take=take):
+                take([2 * i, 2 * i + 1])
+                return carry
+
+            lax.fori_loop(0, count // 2, pair, 0)
+        if count % 2:
+            take([count - 1])
 
     if last:
         squares = jnp.zeros((8, rows), jnp.float32)
@@ -217,11 +235,12 @@
         out_specs = (VMEM,) * 3
         if first:
             out_shape = (
-                jax.ShapeDtypeStruct((5,), jnp.int32),
+                jax.ShapeDtypeStruct((4,), jnp.int32),
+                jax.ShapeDtypeStruct((1, rows), jnp.int32),
                 jax.ShapeDtypeStruct((1, width), jnp.float32),
                 jax.ShapeDtypeStruct((8, width), jnp.bfloat16),
             ) + out_shape
-            out_specs = (SMEM, VMEM, VMEM) + out_specs
+            out_specs = (SMEM, VMEM, VMEM, VMEM) + out_specs
     pairs = sum(p[0] for p in plan) * blocks[0].shape[2] * rows * heads
     return pl.pallas_call(
         functools.partial(attend_kernel, plan, first, last, members),
@@ -237,10 +256,10 @@
     )(*operands)
 
 
-def finish_kernel(branches, meta_ref, everyone, scaled_ref, normed_ref, joined_ref):
+def finish_kernel(branches, side_ref, everyone, scaled_ref, normed_ref, joined_ref):
     rows, width = scaled_ref.shape
     size = everyone.shape[0] // branches
-    mine = meta_ref[4]
+    mine = side_ref[...]
     joined = jnp.zeros((1, rows), jnp.float32)
     own = jnp.zeros((1, rows), jnp.float32)
     for b in range(branches):
@@ -269,7 +288,7 @@
     from_1 = moved(own, lambda x, y, c: (x + 1, y, c))
     from_2 = moved(own, lambda x, y, c: (x + 2, y, c))
 
-    meta, gain, pieces, *state = attend(
+    meta, side, gain, pieces, *state = attend(
         [
             here.reshape(1),
             lax.axis_index("branch").reshape(1),
@@ -307,11 +326,11 @@
             jax.ShapeDtypeStruct((rows, width), jnp.bfloat16),
             jax.ShapeDtypeStruct((1, rows), jnp.float32),
         ),
-        in_specs=[SMEM] + [VMEM] * 2,
+        in_specs=[VMEM] * 3,
         out_specs=(VMEM,) * 2,
         compiler_params=SMALL,
         name="finish",
-    )(meta, everyone, scaled)
+    )(side, everyone, scaled)
     return (normed[None], joined[0])
 
 

time: 89.2 us -> 90.4 us (1.013)
  the two profiles are of different devices: /device:TPU:31 before, /device:TPU:7 now
where the time goes in v2:
time: 90.4 us; the launch traced here: 90 us
  blocking collectives  25.6 us (28%)
  starting transfers between devices  23 us (25%)
  Pallas kernels  21.9 us (24%)
  waiting for transfers between devices  16.9 us (19%)
  other arithmetic  1.03 us (1%)
    all_to_all x1, blocking collectives, local(): everyone = lax.all_to_all(stats, ('branch', 'tp'), 0, 0, tiled=True)  25.6 us
    ppermute x8, starting transfers between devices, moved(): return lax.ppermute(block, 'ctx', route)  23 us
    pallas_call x7, Pallas kernels, attend(): pl.pallas_call(functools.partial(attend_kernel, plan, first, last, member...  20.9 us
    ppermute x8, waiting for transfers between devices, moved(): return lax.ppermute(block, 'ctx', route)  16.9 us
  transfers between devices with their start and end apart: 8, of which 3 were waited for; matrix products, arithmetic and copies ran while one was open for 0% of the time, Pallas kernels for 20%

profile of v2, /device:TPU:7, one launch (start us, length us, event | category | flops | bytes accessed | tf_op | source)
XLA Modules:
  0.0 90.0 jit_solution(12898232223215993611)
XLA Ops:
  0.6 0.9 maximum_bitcast_fusion.refs_6_
  1.5 1.3 %collective-permute-start.1 = (bf16[1,2,256,128]{3,2,1,0:T(8,128)(2,1)S(1)}, bf16[1,2,256,128]{3,2,1,0:T(8,128)(2,1)S(1)}, u32[]{:S(2)}, u32[]{:S(2)}) collective-permute-start(bf16[1,2,256,128]{3,2,1,0:T(8,128)(2,1)S(1)} %maximum_bitcast_fusion.refs_6_), channel_id=1, source_target_pairs={{0,128},{8,136},{16,144},{24,152},{32,160},{40,168},{48,176},{56,1... | collective-permute-start | bytes 393224 | tf_op jit(solution)/shard_map/ppermute | solution.py:39
  2.8 1.3 %collective-permute-start = (bf16[1,2,256,128]{3,2,1,0:T(8,128)(2,1)S(1)}, bf16[1,2,256,128]{3,2,1,0:T(8,128)(2,1)S(1)}, u32[]{:S(2)}, u32[]{:S(2)}) collective-permute-start(bf16[1,2,256,128]{3,2,1,0:T(8,128)(2,1)S(1)} %maximum_bitcast_fusion.refs_6_), channel_id=1, source_target_pairs={{0,64},{8,72},{16,80},{24,88},{32,96},{40,104},{48,112},{56,120},{... | collective-permute-start | bytes 393224 | tf_op jit(solution)/shard_map/ppermute | solution.py:39
  4.1 5.2 %collective-permute-done.1 = bf16[1,2,256,128]{3,2,1,0:T(8,128)(2,1)S(1)} collective-permute-done((bf16[1,2,256,128]{3,2,1,0:T(8,128)(2,1)S(1)}, bf16[1,2,256,128]{3,2,1,0:T(8,128)(2,1)S(1)}, u32[]{:S(2)}, u32[]{:S(2)}) %collective-permute-start.1) | collective-permute-done | bytes 131104 | tf_op jit(solution)/shard_map/ppermute | solution.py:39
  9.3 0.0 collective-permute-done
  9.4 3.2 %collective-permute-start.5 = (bf16[2,2,256,128]{3,2,1,0:T(8,128)(2,1)S(1)}, bf16[2,2,256,128]{3,2,1,0:T(8,128)(2,1)S(1)}, u32[]{:S(2)}, u32[]{:S(2)}) collective-permute-start(bf16[2,2,256,128]{3,2,1,0:T(8,128)(2,1)S(1)} %get-tuple-element.54), channel_id=1, source_target_pairs={{0,16},{8,24},{16,0},{24,8},{32,48},{40,56},{48,32},{56,40},{64,80... | collective-permute-start | bytes 786440 | tf_op jit(solution)/shard_map/ppermute | solution.py:39
  12.6 4.2 %collective-permute-start.2 = (bf16[2,2,256,128]{3,2,1,0:T(8,128)(2,1)S(1)}, bf16[2,2,256,128]{3,2,1,0:T(8,128)(2,1)S(1)}, u32[]{:S(2)}, u32[]{:S(2)}) collective-permute-start(bf16[2,2,256,128]{3,2,1,0:T(8,128)(2,1)S(1)} %get-tuple-element.55), channel_id=1, source_target_pairs={{0,32},{8,40},{16,48},{24,56},{32,0},{40,8},{48,16},{56,24},{64,96... | collective-permute-start | bytes 786440 | tf_op jit(solution)/shard_map/ppermute | solution.py:39
  16.9 0.0 copy-start
  16.9 0.0 copy-start.1
  16.9 4.1 %collective-permute-start.7 = (bf16[3,2,256,128]{3,2,1,0:T(8,128)(2,1)S(1)}, bf16[3,2,256,128]{3,2,1,0:T(8,128)(2,1)S(1)}, u32[]{:S(2)}, u32[]{:S(2)}) collective-permute-start(bf16[3,2,256,128]{3,2,1,0:T(8,128)(2,1)S(1)} %pad_maximum_fusion.1.refs_2_), channel_id=1, source_target_pairs={{0,8},{8,0},{16,24},{24,16},{32,40},{40,32},{48,56},{56,48},{64,72... | collective-permute-start | bytes 1179656 | tf_op jit(solution)/shard_map/ppermute | solution.py:39
  21.1 0.0 collective-permute-done.5.refs_2_
  21.1 6.5 %collective-permute-done.2.refs_2_ = bf16[2,2,256,128]{3,2,1,0:T(8,128)(2,1)S(1)} collective-permute-done((bf16[2,2,256,128]{3,2,1,0:T(8,128)(2,1)S(1)}, bf16[2,2,256,128]{3,2,1,0:T(8,128)(2,1)S(1)}, u32[]{:S(2)}, u32[]{:S(2)}) %collective-permute-start.2) | collective-permute-done | bytes 262176 | tf_op jit(solution)/shard_map/ppermute | solution.py:39
  27.6 4.2 %collective-permute-start.6 = (bf16[4,2,256,128]{3,2,1,0:T(8,128)(2,1)S(1)}, bf16[4,2,256,128]{3,2,1,0:T(8,128)(2,1)S(1)}, u32[]{:S(2)}, u32[]{:S(2)}) collective-permute-start(bf16[4,2,256,128]{3,2,1,0:T(8,128)(2,1)S(1)} %pad_maximum_fusion), channel_id=1, source_target_pairs={{0,8},{8,0},{16,24},{24,16},{32,40},{40,32},{48,56},{56,48},{64,72... | collective-permute-start | bytes 1572872 | tf_op jit(solution)/shard_map/ppermute | solution.py:39
  31.8 1.9 %collective-permute-start.3 = (bf16[2,2,256,128]{3,2,1,0:T(8,128)(2,1)S(1)}, bf16[2,2,256,128]{3,2,1,0:T(8,128)(2,1)S(1)}, u32[]{:S(2)}, u32[]{:S(2)}) collective-permute-start(bf16[2,2,256,128]{3,2,1,0:T(8,128)(2,1)S(1)} %collective-permute-done.2.refs_2_), channel_id=1, source_target_pairs={{0,16},{8,24},{16,0},{24,8},{32,48},{40,56},{48,32},{56,40},{64,80... | collective-permute-start | bytes 786440 | tf_op jit(solution)/shard_map/ppermute | solution.py:39
  33.7 0.0 copy-start.3
  33.7 0.0 copy-start.2
  33.7 0.6 copy-done.3
  34.4 0.0 copy-done.2
  34.4 1.9 %attend.7 = (s32[4]{0:T(128)S(1)}, s32[1,256]{1,0:T(1,128)S(1)}, f32[1,1024]{1,0:T(1,128)S(1)}, bf16[8,1024]{1,0:T(8,128)(2,1)S(1)}, f32[8,8,256]{2,1,0:T(8,128)...) custom-call(s32[1]{0:T(128)} %bitcast.refs_0_, s32[1]{0:T(128)} %bitcast.1.refs_1_, f32[1,1024]{1,0:T(1,128)S(1)} %copy-done.2, ...), custom_call_target="tpu_custom_call" | custom-call | flops 268435456 | bytes 1048576 | tf_op jit(solution)/shard_map/attend/pallas_call | solution.py:245
  36.3 5.2 %collective-permute-done.3.refs_2_ = bf16[2,2,256,128]{3,2,1,0:T(8,128)(2,1)S(1)} collective-permute-done((bf16[2,2,256,128]{3,2,1,0:T(8,128)(2,1)S(1)}, bf16[2,2,256,128]{3,2,1,0:T(8,128)(2,1)S(1)}, u32[]{:S(2)}, u32[]{:S(2)}) %collective-permute-start.3) | collective-permute-done | bytes 262176 | tf_op jit(solution)/shard_map/ppermute | solution.py:39
  41.5 2.8 %collective-permute-start.4 = (bf16[2,2,256,128]{3,2,1,0:T(8,128)(2,1)S(1)}, bf16[2,2,256,128]{3,2,1,0:T(8,128)(2,1)S(1)}, u32[]{:S(2)}, u32[]{:S(2)}) collective-permute-start(bf16[2,2,256,128]{3,2,1,0:T(8,128)(2,1)S(1)} %collective-permute-done.3.refs_2_), channel_id=1, source_target_pairs={{0,8},{8,0},{16,24},{24,16},{32,40},{40,32},{48,56},{56,48},{64,72... | collective-permute-start | bytes 786440 | tf_op jit(solution)/shard_map/ppermute | solution.py:39
  44.3 0.0 collective-permute-done.7.refs_3_
  44.3 5.1 %attend.8 = (f32[8,8,256]{2,1,0:T(8,128)S(1)}, f32[8,8,256]{2,1,0:T(8,128)S(1)}, f32[8,128,256]{2,1,0:T(8,128)S(1)}) custom-call(s32[4]{0:T(128)S(1)} %get-tuple-element.29.refs_0_, bf16[256,1024]{1,0:T(8,128)(2,1)S(1)} %bitcast.9, bf16[3,2,256,128]{3,2,1,0:T(8,128)(2,1)S(1)} %pad_maximum_fusion.1.refs_2_, ...), custom_call_target="tpu_custom_call" | custom-call | flops 1342177280 | bytes 1048576 | tf_op jit(solution)/shard_map/attend/pallas_call | solution.py:245
  49.4 2.5 %attend.9 = (f32[8,8,256]{2,1,0:T(8,128)S(1)}, f32[8,8,256]{2,1,0:T(8,128)S(1)}, f32[8,128,256]{2,1,0:T(8,128)S(1)}) custom-call(s32[4]{0:T(128)S(1)} %get-tuple-element.29.refs_0_, bf16[256,1024]{1,0:T(8,128)(2,1)S(1)} %bitcast.10, bf16[2,2,256,128]{3,2,1,0:T(8,128)(2,1)S(1)} %collective-permute-done.5.refs_2_, f32[8,8,256]{2,1,0:T(8,128)S(1)} %get-tuple-element.33.refs_3_, ...), custom_call_target="tpu_custom_call" | custom-call | flops 536870912 | bytes 1048576 | tf_op jit(solution)/shard_map/attend/pallas_call | solution.py:245
  51.9 2.3 %attend.10 = (f32[8,8,256]{2,1,0:T(8,128)S(1)}, f32[8,8,256]{2,1,0:T(8,128)S(1)}, f32[8,128,256]{2,1,0:T(8,128)S(1)}) custom-call(s32[4]{0:T(128)S(1)} %get-tuple-element.29.refs_0_, bf16[256,1024]{1,0:T(8,128)(2,1)S(1)} %bitcast.11, bf16[2,2,256,128]{3,2,1,0:T(8,128)(2,1)S(1)} %collective-permute-done.2.refs_2_, ...), custom_call_target="tpu_custom_call" | custom-call | flops 536870912 | bytes 1048576 | tf_op jit(solution)/shard_map/attend/pallas_call | solution.py:245
  54.2 0.0 collective-permute-done.6.refs_2_
  54.3 4.2 %attend.11 = (f32[8,8,256]{2,1,0:T(8,128)S(1)}, f32[8,8,256]{2,1,0:T(8,128)S(1)}, f32[8,128,256]{2,1,0:T(8,128)S(1)}) custom-call(s32[4]{0:T(128)S(1)} %get-tuple-element.29.refs_0_, bf16[256,1024]{1,0:T(8,128)(2,1)S(1)} %bitcast.12, bf16[4,2,256,128]{3,2,1,0:T(8,128)(2,1)S(1)} %collective-permute-done.6.refs_2_, ...), custom_call_target="tpu_custom_call" | custom-call | flops 1073741824 | bytes 1048576 | tf_op jit(solution)/shard_map/attend/pallas_call | solution.py:245
  58.4 2.3 %attend.12 = (f32[8,8,256]{2,1,0:T(8,128)S(1)}, f32[8,8,256]{2,1,0:T(8,128)S(1)}, f32[8,128,256]{2,1,0:T(8,128)S(1)}) custom-call(s32[4]{0:T(128)S(1)} %get-tuple-element.29.refs_0_, bf16[256,1024]{1,0:T(8,128)(2,1)S(1)} %bitcast.13, bf16[2,2,256,128]{3,2,1,0:T(8,128)(2,1)S(1)} %collective-permute-done.3.refs_2_, ...), custom_call_target="tpu_custom_call" | custom-call | flops 536870912 | bytes 1048576 | tf_op jit(solution)/shard_map/attend/pallas_call | solution.py:245
  60.8 0.0 collective-permute-done.4.refs_2_
  60.8 2.6 %attend.13 = (f32[256,1024]{1,0:T(8,128)S(1)}, f32[16,1,512]{2,1,0:T(1,128)S(1)}) custom-call(s32[4]{0:T(128)S(1)} %get-tuple-element.29.refs_0_, bf16[256,1024]{1,0:T(8,128)(2,1)S(1)} %bitcast.14, bf16[2,2,256,128]{3,2,1,0:T(8,128)(2,1)S(1)} %collective-permute-done.4.refs_2_, f32[8,8,256]{2,1,0:T(8,128)S(1)} %get-tuple-element.45.refs_3_, ...), custom_call_target="tpu_custom_call" | custom-call | flops 536870912 | bytes 1048576 | tf_op jit(solution)/shard_map/attend/pallas_call | solution.py:245
  63.4 25.6 %all_to_all.5.everyone = f32[16,1,512]{2,1,0:T(1,128)S(1)} all-to-all(f32[16,1,512]{2,1,0:T(1,128)S(1)} %get-tuple-element.50), channel_id=1, replica_groups=mesh['branch'=2,'ctx'=32,'tp'=8] {'branch','tp'}, dimensions={0} | all-to-all | bytes 65536 | tf_op jit(solution)/shard_map/all_to_all | solution.py:322
  89.0 1.0 %finish.1 = (bf16[256,1024]{1,0:T(8,128)(2,1)}, f32[1,256]{1,0:T(1,128)}) custom-call(s32[1,256]{1,0:T(1,128)S(1)} %get-tuple-element.28.side_ref, f32[16,1,512]{2,1,0:T(1,128)S(1)} %all_to_all.5.everyone, f32[256,1024]{1,0:T(8,128)S(1)} %get-tuple-element.51.scaled_ref), custom_call_target="tpu_custom_call" | custom-call | tf_op jit(solution)/shard_map/finish/pallas_call | solution.py:323
  (7 shorter events, 0.2 us)
Async XLA Ops:
  1.5 7.8 %collective-permute-start.1 = (bf16[1,2,256,128]{3,2,1,0:T(8,128)(2,1)S(1)}, bf16[1,2,256,128]{3,2,1,0:T(8,128)(2,1)S(1)}, u32[]{:S(2)}, u32[]{:S(2)}) collective-permute-start(bf16[1,2,256,128]{3,2,1,0:T(8,128)(2,1)S(1)} %maximum_bitcast_fusion.refs_6_), channel_id=1, source_target_pairs={{0,128},{8,136},{16,144},{24,152},{32,160},{40,168},{48,176},{56,1... | collective-permute-start | bytes 393224 | tf_op jit(solution)/shard_map/ppermute | solution.py:39
  2.8 6.5 %collective-permute-start = (bf16[1,2,256,128]{3,2,1,0:T(8,128)(2,1)S(1)}, bf16[1,2,256,128]{3,2,1,0:T(8,128)(2,1)S(1)}, u32[]{:S(2)}, u32[]{:S(2)}) collective-permute-start(bf16[1,2,256,128]{3,2,1,0:T(8,128)(2,1)S(1)} %maximum_bitcast_fusion.refs_6_), channel_id=1, source_target_pairs={{0,64},{8,72},{16,80},{24,88},{32,96},{40,104},{48,112},{56,120},{... | collective-permute-start | bytes 393224 | tf_op jit(solution)/shard_map/ppermute | solution.py:39
  9.4 11.7 %collective-permute-start.5 = (bf16[2,2,256,128]{3,2,1,0:T(8,128)(2,1)S(1)}, bf16[2,2,256,128]{3,2,1,0:T(8,128)(2,1)S(1)}, u32[]{:S(2)}, u32[]{:S(2)}) collective-permute-start(bf16[2,2,256,128]{3,2,1,0:T(8,128)(2,1)S(1)} %get-tuple-element.54), channel_id=1, source_target_pairs={{0,16},{8,24},{16,0},{24,8},{32,48},{40,56},{48,32},{56,40},{64,80... | collective-permute-start | bytes 786440 | tf_op jit(solution)/shard_map/ppermute | solution.py:39
  12.6 14.9 %collective-permute-start.2 = (bf16[2,2,256,128]{3,2,1,0:T(8,128)(2,1)S(1)}, bf16[2,2,256,128]{3,2,1,0:T(8,128)(2,1)S(1)}, u32[]{:S(2)}, u32[]{:S(2)}) collective-permute-start(bf16[2,2,256,128]{3,2,1,0:T(8,128)(2,1)S(1)} %get-tuple-element.55), channel_id=1, source_target_pairs={{0,32},{8,40},{16,48},{24,56},{32,0},{40,8},{48,16},{56,24},{64,96... | collective-permute-start | bytes 786440 | tf_op jit(solution)/shard_map/ppermute | solution.py:39
  16.9 16.8 %copy-start = (bf16[1,256,1024]{2,1,0:T(8,128)(2,1)S(1)}, bf16[1,256,1024]{2,1,0:T(8,128)(2,1)}, u32[]{:S(2)}) copy-start(bf16[1,256,1024]{2,1,0:T(8,128)(2,1)} %param.6) | copy-start | bytes 1572868
  16.9 16.8 %copy-start.1 = (s32[8192]{0:T(1024)S(1)}, s32[8192]{0:T(1024)}, u32[]{:S(2)}) copy-start(s32[8192]{0:T(1024)} %param.9) | copy-start | bytes 98308
  16.9 27.4 %collective-permute-start.7 = (bf16[3,2,256,128]{3,2,1,0:T(8,128)(2,1)S(1)}, bf16[3,2,256,128]{3,2,1,0:T(8,128)(2,1)S(1)}, u32[]{:S(2)}, u32[]{:S(2)}) collective-permute-start(bf16[3,2,256,128]{3,2,1,0:T(8,128)(2,1)S(1)} %pad_maximum_fusion.1.refs_2_), channel_id=1, source_target_pairs={{0,8},{8,0},{16,24},{24,16},{32,40},{40,32},{48,56},{56,48},{64,72... | collective-permute-start | bytes 1179656 | tf_op jit(solution)/shard_map/ppermute | solution.py:39
  27.6 26.7 %collective-permute-start.6 = (bf16[4,2,256,128]{3,2,1,0:T(8,128)(2,1)S(1)}, bf16[4,2,256,128]{3,2,1,0:T(8,128)(2,1)S(1)}, u32[]{:S(2)}, u32[]{:S(2)}) collective-permute-start(bf16[4,2,256,128]{3,2,1,0:T(8,128)(2,1)S(1)} %pad_maximum_fusion), channel_id=1, source_target_pairs={{0,8},{8,0},{16,24},{24,16},{32,40},{40,32},{48,56},{56,48},{64,72... | collective-permute-start | bytes 1572872 | tf_op jit(solution)/shard_map/ppermute | solution.py:39
  31.8 9.7 %collective-permute-start.3 = (bf16[2,2,256,128]{3,2,1,0:T(8,128)(2,1)S(1)}, bf16[2,2,256,128]{3,2,1,0:T(8,128)(2,1)S(1)}, u32[]{:S(2)}, u32[]{:S(2)}) collective-permute-start(bf16[2,2,256,128]{3,2,1,0:T(8,128)(2,1)S(1)} %collective-permute-done.2.refs_2_), channel_id=1, source_target_pairs={{0,16},{8,24},{16,0},{24,8},{32,48},{40,56},{48,32},{56,40},{64,80... | collective-permute-start | bytes 786440 | tf_op jit(solution)/shard_map/ppermute | solution.py:39
  33.7 0.7 copy-start.3
  33.7 0.7 copy-start.2
  41.5 19.3 %collective-permute-start.4 = (bf16[2,2,256,128]{3,2,1,0:T(8,128)(2,1)S(1)}, bf16[2,2,256,128]{3,2,1,0:T(8,128)(2,1)S(1)}, u32[]{:S(2)}, u32[]{:S(2)}) collective-permute-start(bf16[2,2,256,128]{3,2,1,0:T(8,128)(2,1)S(1)} %collective-permute-done.3.refs_2_), channel_id=1, source_target_pairs={{0,8},{8,0},{16,24},{24,16},{32,40},{40,32},{48,56},{56,48},{64,72... | collective-permute-start | bytes 786440 | tf_op jit(solution)/shard_map/ppermute | solution.py:39

commit v3 on v2

--- a/solution.py
+++ b/solution.py
@@ -54,15 +54,22 @@
         gain_ref, pieces_ref = refs[:2]
         scaled_ref, stats_ref, m_ref, l_ref, acc_ref = refs[2:]
     elif first:
-        meta_ref, side_ref, held_gain_ref, pieces_ref, m_ref, l_ref, acc_ref = refs
+        meta_ref, parts_ref, side_ref, held_gain_ref, pieces_ref, m_ref, l_ref, acc_ref = refs
     else:
         m_ref, l_ref, acc_ref = refs
     rows = q_ref.shape[0]
-    heads = q_ref.shape[1] // HD
+    heads = q_ref.shape[1] // (HD if first else 2 * HD)
     keys = kv_refs[0].shape[2]
     factor = math.log2(math.e) / math.sqrt(HD)
 
     if first:
+        for g in range(heads):
+            scaled = q_ref[:, g * HD : (g + 1) * HD].astype(jnp.float32) * factor
+            high_part = scaled.astype(jnp.bfloat16)
+            low_part = (scaled - high_part.astype(jnp.float32)).astype(jnp.bfloat16)
+            parts_ref[:, 2 * g * HD : (2 * g + 1) * HD] = high_part
+            parts_ref[:, (2 * g + 1) * HD : 2 * (g + 1) * HD] = low_part
+        q_ref = parts_ref
         here = here_ref[0]
         segments = segments_ref[...]
         meta_ref[0] = here
@@ -108,6 +115,7 @@
         join = lambda n: jnp.concatenate([kv_ref[j, n] for j in entries], axis=0)
         key_rows, value_rows = join(0), join(1)
         keys = key_rows.shape[0]
+        key_twice = jnp.concatenate([key_rows, key_rows], axis=1)
         tall = jnp.concatenate([value_rows.T, jnp.ones((16, keys), jnp.bfloat16)], axis=0)
         if masked:
             within = lax.broadcasted_iota(jnp.int32, (rows, rows), 0)
@@ -117,8 +125,8 @@
 
         def scores_of(g):
             return lax.dot_general(
-                key_rows,
-                q_ref[:, g * HD : (g + 1) * HD],
+                key_twice,
+                q_ref[:, 2 * g * HD : 2 * (g + 1) * HD],
                 (((1,), (1,)), ((), ())),
                 preferred_element_type=jnp.float32,
             )
@@ -142,8 +150,8 @@
             top = jnp.max(jnp.max(scores, axis=0), axis=0, keepdims=True)
             new = jnp.maximum(old, jnp.broadcast_to(top, old.shape))
             m_ref[g] = new
-            rescale = jnp.exp2((old - new) * factor)
-            weights = jnp.exp2((scores - new[None]) * factor)
+            rescale = jnp.exp2(old - new)
+            weights = jnp.exp2(scores - new[None])
             waiting.append((g, weights.reshape(keys, rows).astype(jnp.bfloat16), rescale))
             if len(waiting) > BEHIND:
                 mix(*waiting.pop(0))
@@ -217,8 +225,9 @@
 
 def attend(operands, blocks, plan, state=None, gains=None, members=0):
     first, last = state is None, gains is not None
-    rows, width = operands[-1].shape
-    heads = width // HD
+    rows = operands[-1].shape[0]
+    heads = operands[-1].shape[1] // (HD if first else 2 * HD)
+    width = heads * HD
     state_shapes = [(heads, 8, rows), (heads, 8, rows), (heads, HD, rows)]
     operands = [*operands, *blocks, *(state or ()), *(gains or ())]
     scratch = []
@@ -236,11 +245,12 @@
         if first:
             out_shape = (
                 jax.ShapeDtypeStruct((4,), jnp.int32),
+                jax.ShapeDtypeStruct((rows, 2 * width), jnp.bfloat16),
                 jax.ShapeDtypeStruct((1, rows), jnp.int32),
                 jax.ShapeDtypeStruct((1, width), jnp.float32),
                 jax.ShapeDtypeStruct((8, width), jnp.bfloat16),
             ) + out_shape
-            out_specs = (SMEM, VMEM, VMEM, VMEM) + out_specs
+            out_specs = (SMEM, VMEM, VMEM, VMEM, VMEM) + out_specs
     pairs = sum(p[0] for p in plan) * blocks[0].shape[2] * rows * heads
     return pl.pallas_call(
         functools.partial(attend_kernel, plan, first, last, members),
@@ -288,7 +298,7 @@
     from_1 = moved(own, lambda x, y, c: (x + 1, y, c))
     from_2 = moved(own, lambda x, y, c: (x + 2, y, c))
 
-    meta, side, gain, pieces, *state = attend(
+    meta, parts, side, gain, pieces, *state = attend(
         [
             here.reshape(1),
             lax.axis_index("branch").reshape(1),
@@ -305,19 +315,21 @@
     across_2 = moved(pick(y < 2), lambda x, y, c: (x, y ^ 2, c))
     across_1 = moved(pick((y & 1) == 0), lambda x, y, c: (x, y ^ 1, c))
     column_p = partner(column)
-    state = attend([meta, q], [column, column_p], ((2, -2, 0, 0), (3, -2, 0, 1)), state)
-    state = attend([meta, q], [across_1], ((2, None, 1, 0),), state)
+    state = attend(
+        [meta, parts], [column, column_p], ((2, -2, 0, 0), (3, -2, 0, 1)), state
+    )
+    state = attend([meta, parts], [across_1], ((2, None, 1, 0),), state)
     across_3 = moved(across_2, lambda x, y, c: (x, y ^ 1, c))
     near = jnp.concatenate([across_1, across_2])
     near_p = partner(near)
-    state = attend([meta, q], [across_2], ((2, None, 2, 0),), state)
-    state = attend([meta, q], [near_p], ((4, None, (1, 2), 1),), state)
+    state = attend([meta, parts], [across_2], ((2, None, 2, 0),), state)
+    state = attend([meta, parts], [near_p], ((4, None, (1, 2), 1),), state)
     across_3p = partner(across_3)
-    state = attend([meta, q], [across_3], ((2, None, 3, 0),), state)
+    state = attend([meta, parts], [across_3], ((2, None, 3, 0),), state)
     branches = lax.axis_size("branch")
     members = branches * lax.axis_size("tp")
     scaled, stats = attend(
-        [meta, q], [across_3p], ((2, None, 3, 1),), state, (gain, pieces), members
+        [meta, parts], [across_3p], ((2, None, 3, 1),), state, (gain, pieces), members
     )
     everyone = lax.all_to_all(stats, ("branch", "tp"), 0, 0, tiled=True)
     normed, joined = pl.pallas_call(

time: 90.4 us -> 89.6 us (level)
  no operation moved by 1% of the time
where the time goes in v3:
time: 89.6 us; the launch traced here: 89.2 us
  blocking collectives  25.7 us (29%)
  starting transfers between devices  23 us (26%)
  Pallas kernels  21.3 us (24%)
  waiting for transfers between devices  16.6 us (19%)
  other arithmetic  1.03 us (1%)
    all_to_all x1, blocking collectives, local(): everyone = lax.all_to_all(stats, ('branch', 'tp'), 0, 0, tiled=True)  25.7 us
    ppermute x8, starting transfers between devices, moved(): return lax.ppermute(block, 'ctx', route)  23 us
    pallas_call x7, Pallas kernels, attend(): pl.pallas_call(functools.partial(attend_kernel, plan, first, last, member...  20.3 us
    ppermute x8, waiting for transfers between devices, moved(): return lax.ppermute(block, 'ctx', route)  16.6 us
  transfers between devices with their start and end apart: 8, of which 3 were waited for; matrix products, arithmetic and copies ran while one was open for 0% of the time, Pallas kernels for 20%

profile of v3, /device:TPU:7, one launch (start us, length us, event | category | flops | bytes accessed | tf_op | source)
XLA Modules:
  0.0 89.2 jit_solution(10201946657906347387)
XLA Ops:
  0.6 0.9 maximum_bitcast_fusion.refs_6_
  1.5 1.3 %collective-permute-start.1 = (bf16[1,2,256,128]{3,2,1,0:T(8,128)(2,1)S(1)}, bf16[1,2,256,128]{3,2,1,0:T(8,128)(2,1)S(1)}, u32[]{:S(2)}, u32[]{:S(2)}) collective-permute-start(bf16[1,2,256,128]{3,2,1,0:T(8,128)(2,1)S(1)} %maximum_bitcast_fusion.refs_6_), channel_id=1, source_target_pairs={{0,128},{8,136},{16,144},{24,152},{32,160},{40,168},{48,176},{56,1... | collective-permute-start | bytes 393224 | tf_op jit(solution)/shard_map/ppermute | solution.py:39
  2.8 1.3 %collective-permute-start = (bf16[1,2,256,128]{3,2,1,0:T(8,128)(2,1)S(1)}, bf16[1,2,256,128]{3,2,1,0:T(8,128)(2,1)S(1)}, u32[]{:S(2)}, u32[]{:S(2)}) collective-permute-start(bf16[1,2,256,128]{3,2,1,0:T(8,128)(2,1)S(1)} %maximum_bitcast_fusion.refs_6_), channel_id=1, source_target_pairs={{0,64},{8,72},{16,80},{24,88},{32,96},{40,104},{48,112},{56,120},{... | collective-permute-start | bytes 393224 | tf_op jit(solution)/shard_map/ppermute | solution.py:39
  4.1 5.2 %collective-permute-done.1 = bf16[1,2,256,128]{3,2,1,0:T(8,128)(2,1)S(1)} collective-permute-done((bf16[1,2,256,128]{3,2,1,0:T(8,128)(2,1)S(1)}, bf16[1,2,256,128]{3,2,1,0:T(8,128)(2,1)S(1)}, u32[]{:S(2)}, u32[]{:S(2)}) %collective-permute-start.1) | collective-permute-done | bytes 131104 | tf_op jit(solution)/shard_map/ppermute | solution.py:39
  9.3 0.0 collective-permute-done
  9.4 3.2 %collective-permute-start.5 = (bf16[2,2,256,128]{3,2,1,0:T(8,128)(2,1)S(1)}, bf16[2,2,256,128]{3,2,1,0:T(8,128)(2,1)S(1)}, u32[]{:S(2)}, u32[]{:S(2)}) collective-permute-start(bf16[2,2,256,128]{3,2,1,0:T(8,128)(2,1)S(1)} %get-tuple-element.56), channel_id=1, source_target_pairs={{0,16},{8,24},{16,0},{24,8},{32,48},{40,56},{48,32},{56,40},{64,80... | collective-permute-start | bytes 786440 | tf_op jit(solution)/shard_map/ppermute | solution.py:39
  12.6 4.2 %collective-permute-start.2 = (bf16[2,2,256,128]{3,2,1,0:T(8,128)(2,1)S(1)}, bf16[2,2,256,128]{3,2,1,0:T(8,128)(2,1)S(1)}, u32[]{:S(2)}, u32[]{:S(2)}) collective-permute-start(bf16[2,2,256,128]{3,2,1,0:T(8,128)(2,1)S(1)} %get-tuple-element.57), channel_id=1, source_target_pairs={{0,32},{8,40},{16,48},{24,56},{32,0},{40,8},{48,16},{56,24},{64,96... | collective-permute-start | bytes 786440 | tf_op jit(solution)/shard_map/ppermute | solution.py:39
  16.9 0.0 copy-start
  16.9 0.0 copy-start.1
  16.9 4.1 %collective-permute-start.7 = (bf16[3,2,256,128]{3,2,1,0:T(8,128)(2,1)S(1)}, bf16[3,2,256,128]{3,2,1,0:T(8,128)(2,1)S(1)}, u32[]{:S(2)}, u32[]{:S(2)}) collective-permute-start(bf16[3,2,256,128]{3,2,1,0:T(8,128)(2,1)S(1)} %pad_maximum_fusion.1.refs_2_), channel_id=1, source_target_pairs={{0,8},{8,0},{16,24},{24,16},{32,40},{40,32},{48,56},{56,48},{64,72... | collective-permute-start | bytes 1179656 | tf_op jit(solution)/shard_map/ppermute | solution.py:39
  21.1 0.0 collective-permute-done.5.refs_2_
  21.1 6.5 %collective-permute-done.2.refs_2_ = bf16[2,2,256,128]{3,2,1,0:T(8,128)(2,1)S(1)} collective-permute-done((bf16[2,2,256,128]{3,2,1,0:T(8,128)(2,1)S(1)}, bf16[2,2,256,128]{3,2,1,0:T(8,128)(2,1)S(1)}, u32[]{:S(2)}, u32[]{:S(2)}) %collective-permute-start.2) | collective-permute-done | bytes 262176 | tf_op jit(solution)/shard_map/ppermute | solution.py:39
  27.6 4.2 %collective-permute-start.6 = (bf16[4,2,256,128]{3,2,1,0:T(8,128)(2,1)S(1)}, bf16[4,2,256,128]{3,2,1,0:T(8,128)(2,1)S(1)}, u32[]{:S(2)}, u32[]{:S(2)}) collective-permute-start(bf16[4,2,256,128]{3,2,1,0:T(8,128)(2,1)S(1)} %pad_maximum_fusion), channel_id=1, source_target_pairs={{0,8},{8,0},{16,24},{24,16},{32,40},{40,32},{48,56},{56,48},{64,72... | collective-permute-start | bytes 1572872 | tf_op jit(solution)/shard_map/ppermute | solution.py:39
  31.8 1.9 %collective-permute-start.3 = (bf16[2,2,256,128]{3,2,1,0:T(8,128)(2,1)S(1)}, bf16[2,2,256,128]{3,2,1,0:T(8,128)(2,1)S(1)}, u32[]{:S(2)}, u32[]{:S(2)}) collective-permute-start(bf16[2,2,256,128]{3,2,1,0:T(8,128)(2,1)S(1)} %collective-permute-done.2.refs_2_), channel_id=1, source_target_pairs={{0,16},{8,24},{16,0},{24,8},{32,48},{40,56},{48,32},{56,40},{64,80... | collective-permute-start | bytes 786440 | tf_op jit(solution)/shard_map/ppermute | solution.py:39
  33.7 0.0 copy-start.3
  33.7 0.0 copy-start.2
  33.7 0.6 copy-done.3
  34.4 0.0 copy-done.2
  34.4 2.1 %attend.7 = (s32[4]{0:T(128)S(1)}, bf16[256,2048]{1,0:T(8,128)(2,1)S(1)}, s32[1,256]{1,0:T(1,128)S(1)}, f32[1,1024]{1,0:T(1,128)S(1)}, bf16[8,1024]{1,0:T(8,128)...) custom-call(s32[1]{0:T(128)} %bitcast.refs_0_, s32[1]{0:T(128)} %bitcast.1.refs_1_, ...), custom_call_target="tpu_custom_call" | custom-call | flops 268435456 | bytes 1048576 | tf_op jit(solution)/shard_map/attend/pallas_call | solution.py:255
  36.5 5.0 %collective-permute-done.3.refs_2_ = bf16[2,2,256,128]{3,2,1,0:T(8,128)(2,1)S(1)} collective-permute-done((bf16[2,2,256,128]{3,2,1,0:T(8,128)(2,1)S(1)}, bf16[2,2,256,128]{3,2,1,0:T(8,128)(2,1)S(1)}, u32[]{:S(2)}, u32[]{:S(2)}) %collective-permute-start.3) | collective-permute-done | bytes 262176 | tf_op jit(solution)/shard_map/ppermute | solution.py:39
  41.5 2.8 %collective-permute-start.4 = (bf16[2,2,256,128]{3,2,1,0:T(8,128)(2,1)S(1)}, bf16[2,2,256,128]{3,2,1,0:T(8,128)(2,1)S(1)}, u32[]{:S(2)}, u32[]{:S(2)}) collective-permute-start(bf16[2,2,256,128]{3,2,1,0:T(8,128)(2,1)S(1)} %collective-permute-done.3.refs_2_), channel_id=1, source_target_pairs={{0,8},{8,0},{16,24},{24,16},{32,40},{40,32},{48,56},{56,48},{64,72... | collective-permute-start | bytes 786440 | tf_op jit(solution)/shard_map/ppermute | solution.py:39
  44.3 0.0 collective-permute-done.7.refs_3_
  44.3 4.8 %attend.8 = (f32[8,8,256]{2,1,0:T(8,128)S(1)}, f32[8,8,256]{2,1,0:T(8,128)S(1)}, f32[8,128,256]{2,1,0:T(8,128)S(1)}) custom-call(s32[4]{0:T(128)S(1)} %get-tuple-element.30.refs_0_, bf16[256,2048]{1,0:T(8,128)(2,1)S(1)} %get-tuple-element.31.refs_1_, bf16[3,2,256,128]{3,2,1,0:T(8,128)(2,1)S(1)} %pad_maximum_fusion.1.refs_2_, ...), custom_call_target="tpu_custom_call" | custom-call | flops 1342177280 | bytes 1048576 | tf_op jit(solution)/shard_map/attend/pallas_call | solution.py:255
  49.1 2.4 %attend.9 = (f32[8,8,256]{2,1,0:T(8,128)S(1)}, f32[8,8,256]{2,1,0:T(8,128)S(1)}, f32[8,128,256]{2,1,0:T(8,128)S(1)}) custom-call(s32[4]{0:T(128)S(1)} %get-tuple-element.30.refs_0_, bf16[256,2048]{1,0:T(8,128)(2,1)S(1)} %get-tuple-element.31.refs_1_, bf16[2,2,256,128]{3,2,1,0:T(8,128)(2,1)S(1)} %collective-permute-done.5.refs_2_, ...), custom_call_target="tpu_custom_call" | custom-call | flops 536870912 | bytes 1048576 | tf_op jit(solution)/shard_map/attend/pallas_call | solution.py:255
  51.5 2.2 %attend.10 = (f32[8,8,256]{2,1,0:T(8,128)S(1)}, f32[8,8,256]{2,1,0:T(8,128)S(1)}, f32[8,128,256]{2,1,0:T(8,128)S(1)}) custom-call(s32[4]{0:T(128)S(1)} %get-tuple-element.30.refs_0_, bf16[256,2048]{1,0:T(8,128)(2,1)S(1)} %get-tuple-element.31.refs_1_, bf16[2,2,256,128]{3,2,1,0:T(8,128)(2,1)S(1)} %collective-permute-done.2.refs_2_, ...), custom_call_target="tpu_custom_call" | custom-call | flops 536870912 | bytes 1048576 | tf_op jit(solution)/shard_map/attend/pallas_call | solution.py:255
  53.8 0.0 collective-permute-done.6.refs_2_
  53.8 3.9 %attend.11 = (f32[8,8,256]{2,1,0:T(8,128)S(1)}, f32[8,8,256]{2,1,0:T(8,128)S(1)}, f32[8,128,256]{2,1,0:T(8,128)S(1)}) custom-call(s32[4]{0:T(128)S(1)} %get-tuple-element.30.refs_0_, bf16[256,2048]{1,0:T(8,128)(2,1)S(1)} %get-tuple-element.31.refs_1_, bf16[4,2,256,128]{3,2,1,0:T(8,128)(2,1)S(1)} %collective-permute-done.6.refs_2_, ...), custom_call_target="tpu_custom_call" | custom-call | flops 1073741824 | bytes 1048576 | tf_op jit(solution)/shard_map/attend/pallas_call | solution.py:255
  57.7 2.2 %attend.12 = (f32[8,8,256]{2,1,0:T(8,128)S(1)}, f32[8,8,256]{2,1,0:T(8,128)S(1)}, f32[8,128,256]{2,1,0:T(8,128)S(1)}) custom-call(s32[4]{0:T(128)S(1)} %get-tuple-element.30.refs_0_, bf16[256,2048]{1,0:T(8,128)(2,1)S(1)} %get-tuple-element.31.refs_1_, bf16[2,2,256,128]{3,2,1,0:T(8,128)(2,1)S(1)} %collective-permute-done.3.refs_2_, ...), custom_call_target="tpu_custom_call" | custom-call | flops 536870912 | bytes 1048576 | tf_op jit(solution)/shard_map/attend/pallas_call | solution.py:255
  60.0 0.0 collective-permute-done.4.refs_2_
  60.0 2.5 %attend.13 = (f32[256,1024]{1,0:T(8,128)S(1)}, f32[16,1,512]{2,1,0:T(1,128)S(1)}) custom-call(s32[4]{0:T(128)S(1)} %get-tuple-element.30.refs_0_, bf16[256,2048]{1,0:T(8,128)(2,1)S(1)} %get-tuple-element.31.refs_1_, bf16[2,2,256,128]{3,2,1,0:T(8,128)(2,1)S(1)} %collective-permute-done.4.refs_2_, f32[8,8,256]{2,1,0:T(8,128)S(1)} %get-tuple-element.47.refs_3_, ...), custom_call_target="tpu_custom_call" | custom-call | flops 536870912 | bytes 1048576 | tf_op jit(solution)/shard_map/attend/pallas_call | solution.py:255
  62.5 25.7 %all_to_all.5.everyone = f32[16,1,512]{2,1,0:T(1,128)S(1)} all-to-all(f32[16,1,512]{2,1,0:T(1,128)S(1)} %get-tuple-element.52), channel_id=1, replica_groups=mesh['branch'=2,'ctx'=32,'tp'=8] {'branch','tp'}, dimensions={0} | all-to-all | bytes 65536 | tf_op jit(solution)/shard_map/all_to_all | solution.py:334
  88.2 1.0 %finish.1 = (bf16[256,1024]{1,0:T(8,128)(2,1)}, f32[1,256]{1,0:T(1,128)}) custom-call(s32[1,256]{1,0:T(1,128)S(1)} %get-tuple-element.29.side_ref, f32[16,1,512]{2,1,0:T(1,128)S(1)} %all_to_all.5.everyone, f32[256,1024]{1,0:T(8,128)S(1)} %get-tuple-element.53.scaled_ref), custom_call_target="tpu_custom_call" | custom-call | tf_op jit(solution)/shard_map/finish/pallas_call | solution.py:335
  (7 shorter events, 0.2 us)
Async XLA Ops:
  1.5 7.8 %collective-permute-start.1 = (bf16[1,2,256,128]{3,2,1,0:T(8,128)(2,1)S(1)}, bf16[1,2,256,128]{3,2,1,0:T(8,128)(2,1)S(1)}, u32[]{:S(2)}, u32[]{:S(2)}) collective-permute-start(bf16[1,2,256,128]{3,2,1,0:T(8,128)(2,1)S(1)} %maximum_bitcast_fusion.refs_6_), channel_id=1, source_target_pairs={{0,128},{8,136},{16,144},{24,152},{32,160},{40,168},{48,176},{56,1... | collective-permute-start | bytes 393224 | tf_op jit(solution)/shard_map/ppermute | solution.py:39
  2.8 6.5 %collective-permute-start = (bf16[1,2,256,128]{3,2,1,0:T(8,128)(2,1)S(1)}, bf16[1,2,256,128]{3,2,1,0:T(8,128)(2,1)S(1)}, u32[]{:S(2)}, u32[]{:S(2)}) collective-permute-start(bf16[1,2,256,128]{3,2,1,0:T(8,128)(2,1)S(1)} %maximum_bitcast_fusion.refs_6_), channel_id=1, source_target_pairs={{0,64},{8,72},{16,80},{24,88},{32,96},{40,104},{48,112},{56,120},{... | collective-permute-start | bytes 393224 | tf_op jit(solution)/shard_map/ppermute | solution.py:39
  9.4 11.7 %collective-permute-start.5 = (bf16[2,2,256,128]{3,2,1,0:T(8,128)(2,1)S(1)}, bf16[2,2,256,128]{3,2,1,0:T(8,128)(2,1)S(1)}, u32[]{:S(2)}, u32[]{:S(2)}) collective-permute-start(bf16[2,2,256,128]{3,2,1,0:T(8,128)(2,1)S(1)} %get-tuple-element.56), channel_id=1, source_target_pairs={{0,16},{8,24},{16,0},{24,8},{32,48},{40,56},{48,32},{56,40},{64,80... | collective-permute-start | bytes 786440 | tf_op jit(solution)/shard_map/ppermute | solution.py:39
  12.6 14.9 %collective-permute-start.2 = (bf16[2,2,256,128]{3,2,1,0:T(8,128)(2,1)S(1)}, bf16[2,2,256,128]{3,2,1,0:T(8,128)(2,1)S(1)}, u32[]{:S(2)}, u32[]{:S(2)}) collective-permute-start(bf16[2,2,256,128]{3,2,1,0:T(8,128)(2,1)S(1)} %get-tuple-element.57), channel_id=1, source_target_pairs={{0,32},{8,40},{16,48},{24,56},{32,0},{40,8},{48,16},{56,24},{64,96... | collective-permute-start | bytes 786440 | tf_op jit(solution)/shard_map/ppermute | solution.py:39
  16.9 16.8 %copy-start = (bf16[1,256,1024]{2,1,0:T(8,128)(2,1)S(1)}, bf16[1,256,1024]{2,1,0:T(8,128)(2,1)}, u32[]{:S(2)}) copy-start(bf16[1,256,1024]{2,1,0:T(8,128)(2,1)} %param.6) | copy-start | bytes 1572868
  16.9 16.8 %copy-start.1 = (s32[8192]{0:T(1024)S(1)}, s32[8192]{0:T(1024)}, u32[]{:S(2)}) copy-start(s32[8192]{0:T(1024)} %param.9) | copy-start | bytes 98308
  16.9 27.4 %collective-permute-start.7 = (bf16[3,2,256,128]{3,2,1,0:T(8,128)(2,1)S(1)}, bf16[3,2,256,128]{3,2,1,0:T(8,128)(2,1)S(1)}, u32[]{:S(2)}, u32[]{:S(2)}) collective-permute-start(bf16[3,2,256,128]{3,2,1,0:T(8,128)(2,1)S(1)} %pad_maximum_fusion.1.refs_2_), channel_id=1, source_target_pairs={{0,8},{8,0},{16,24},{24,16},{32,40},{40,32},{48,56},{56,48},{64,72... | collective-permute-start | bytes 1179656 | tf_op jit(solution)/shard_map/ppermute | solution.py:39
  27.6 26.2 %collective-permute-start.6 = (bf16[4,2,256,128]{3,2,1,0:T(8,128)(2,1)S(1)}, bf16[4,2,256,128]{3,2,1,0:T(8,128)(2,1)S(1)}, u32[]{:S(2)}, u32[]{:S(2)}) collective-permute-start(bf16[4,2,256,128]{3,2,1,0:T(8,128)(2,1)S(1)} %pad_maximum_fusion), channel_id=1, source_target_pairs={{0,8},{8,0},{16,24},{24,16},{32,40},{40,32},{48,56},{56,48},{64,72... | collective-permute-start | bytes 1572872 | tf_op jit(solution)/shard_map/ppermute | solution.py:39
  31.8 9.7 %collective-permute-start.3 = (bf16[2,2,256,128]{3,2,1,0:T(8,128)(2,1)S(1)}, bf16[2,2,256,128]{3,2,1,0:T(8,128)(2,1)S(1)}, u32[]{:S(2)}, u32[]{:S(2)}) collective-permute-start(bf16[2,2,256,128]{3,2,1,0:T(8,128)(2,1)S(1)} %collective-permute-done.2.refs_2_), channel_id=1, source_target_pairs={{0,16},{8,24},{16,0},{24,8},{32,48},{40,56},{48,32},{56,40},{64,80... | collective-permute-start | bytes 786440 | tf_op jit(solution)/shard_map/ppermute | solution.py:39
  33.7 0.7 copy-start.3
  33.7 0.7 copy-start.2
  41.5 18.5 %collective-permute-start.4 = (bf16[2,2,256,128]{3,2,1,0:T(8,128)(2,1)S(1)}, bf16[2,2,256,128]{3,2,1,0:T(8,128)(2,1)S(1)}, u32[]{:S(2)}, u32[]{:S(2)}) collective-permute-start(bf16[2,2,256,128]{3,2,1,0:T(8,128)(2,1)S(1)} %collective-permute-done.3.refs_2_), channel_id=1, source_target_pairs={{0,8},{8,0},{16,24},{24,16},{32,40},{40,32},{48,56},{56,48},{64,72... | collective-permute-start | bytes 786440 | tf_op jit(solution)/shard_map/ppermute | solution.py:39
